TPU v7x, 512 devices: a whole 4x4x16 slice. The times are simulated.
512 devices in a mesh: kv: 8 (over x, core), pg: 64 (over y, z).
Axes of the slice: x: 4, y: 4, z: 16, core: 2. Of those that a mesh axis runs over, the one named last changes fastest.
Arguments:
- residual_in: bfloat16 [4096, 1536], P('pg', 'kv'), as said below
- queries: bfloat16 [256, 1536], P('pg', 'kv'), as said below
- prefill_attn: bfloat16 [3840, 1536], P('pg', 'kv'), may hold values from -1.1953125 to 1.1953125
- kv_cache: bfloat16 [1024, 8, 128, 128], P('pg', 'kv'), as said below
- page_table: int32 [256, 4], replicated, may hold values from 0 to 1023, as said below
- lengths: int32 [256], replicated, may hold values from 2 to 512, as said below
- out_weight: bfloat16 [1536, 1536], P('kv'), may hold values from -0.75 to 0.75
- norm_gain_in: float32 [1536], P('kv'), may hold values from 0.25 to 1.75
- norm_gain_out: float32 [1536], P('kv'), may hold values from 0.25 to 1.75
- expert_ids: int32 [4096, 8], P('pg'), may hold values from 0 to 39, all different within a row; in each aligned block of 64 rows (0 to 63, 64 to 127, ...) at most 16 rows name the same one
- route_weight: float32 [4096, 8], P('pg'), may hold values from 0.05 to 1
- slot_table: int32 [40, 2], replicated, may hold values from 0 to 63, as said below
- w_gate_up: bfloat16 [64, 1536, 1024], P('pg', 'kv'), as said below
- w_down: bfloat16 [64, 512, 1536], P('pg', None, 'kv'), as said below
Outputs:
- layer_out: bfloat16 [4096, 1536], P('pg', 'kv')
Inputs may be any that keep to these rules, and one draw needn't show every extreme that they name: `page_table`: every page of 0 to 1023 appears exactly once in the table. `lengths`: some request has exactly 512 cached tokens. `slot_table`: row e lists the slots of expert e; each slot of 0 to 63 belongs to exactly one expert; an expert with a single slot repeats it. `w_gate_up`: slots of the same expert carry equal weights; entries lie within -0.2 and 0.2. `w_down`: slots of the same expert carry equal weights; entries lie within -0.3 and 0.3. `queries`: entries lie within -60 and 60. `kv_cache`: entries lie within -6 and 6. `residual_in`: entries lie within -50 and 50. `expert_ids`: in each aligned block of 64 rows no expert is named more than 16 times.
All inputs are finite; a program needn't handle non-finite values.
Results may differ from a plain program's by a relative error of at most 0.02.
Values may be sent and summed in bfloat16 or wider, within the bound.
A program may use at most 128 MiB of HBM per device.

v0:
```python
import jax
import jax.numpy as jnp
from jax import lax
from jax.sharding import PartitionSpec as P

NEG_FILL = -1e30
EPSILON = 1e-06


def merged_2(array, axis, join):
    gathered = jax.tree.map(
        lambda a, kind: lax.all_gather(a.astype(kind), axis),
        array,
        (jnp.bfloat16, jnp.bfloat16, jnp.bfloat16),
    )

    def take(source):
        return jax.tree.map(
            lambda a, own: lax.dynamic_index_in_dim(a, source, 0, False).astype(own.dtype),
            gathered,
            array,
        )

    return lax.fori_loop(
        1, lax.axis_size(axis), lambda source, state: join(state, take(source)), take(0)
    )


def merge_pair(first, secondary_slot):
    highest = jnp.maximum(first[0], secondary_slot[0])
    scale_a = jnp.exp(first[0] - highest)
    scale_b = jnp.exp(secondary_slot[0] - highest)
    head_count = first[0].shape[1]
    acc_a = first[2].reshape(first[2].shape[0], head_count, -1) * scale_a[:, :, None]
    acc_b = (
        secondary_slot[2].reshape(secondary_slot[2].shape[0], head_count, -1) * scale_b[:, :, None]
    )
    return (
        highest,
        first[1] * scale_a + secondary_slot[1] * scale_b,
        (acc_a + acc_b).reshape(first[2].shape),
    )


def local(
    residual_in,
    queries,
    prefill_attn,
    kv_cache,
    page_table,
    lengths,
    out_weight,
    norm_gain_in,
    norm_gain_out,
    expert_ids,
    route_weight,
    slot_table,
    w_gate_up,
    w_down,
):
    head_dim = kv_cache.shape[3] // 2
    page_len = kv_cache.shape[2]
    pages_here = kv_cache.shape[0]
    kv_here = kv_cache.shape[1]
    own_req = queries.shape[0]
    heads_here = queries.shape[1] // head_dim
    head_group = heads_here // kv_here
    total_req = page_table.shape[0]
    max_pages = page_table.shape[1]
    full_gate_up, full_down = (
        lax.all_gather(w_gate_up, "kv", axis=1, tiled=True),
        lax.all_gather(w_down, "kv", axis=2, tiled=True),
    )
    gathered = lax.all_gather(queries, "pg", axis=0, tiled=True)
    page_ids = lax.axis_index("pg") * pages_here + jnp.arange(pages_here, dtype=jnp.int32)
    flat_table = page_table.reshape(-1)
    entry_index = jnp.arange(flat_table.shape[0], dtype=jnp.int32)
    found = jnp.sum(
        jnp.where(flat_table[None, :] == page_ids[:, None], entry_index[None, :], 0), axis=1
    )
    owner = found // max_pages
    page_slot = found % max_pages
    owner_len = lengths[owner]
    query_pages = gathered[owner].reshape(pages_here, kv_here, head_group, head_dim)
    keys = kv_cache[:, :, :, :head_dim]
    values = kv_cache[:, :, :, head_dim:]
    scores = jnp.einsum(
        "pkgd,pktd->pkgt", query_pages, keys, preferred_element_type=jnp.float32
    ) * head_dim ** (-0.5)
    positions = page_slot[:, None] * page_len + jnp.arange(page_len, dtype=jnp.int32)[None, :]
    live = (positions < owner_len[:, None])[:, None, None, :]
    masked = jnp.where(live, scores, NEG_FILL)
    page_top = jnp.max(masked, axis=3)
    probs = jnp.where(live, jnp.exp(masked - page_top[..., None]), 0.0).astype(jnp.bfloat16)
    page_sum = jnp.sum(probs.astype(jnp.float32), axis=3).reshape(pages_here, heads_here)
    page_acc = jnp.einsum(
        "pkgt,pktd->pkgd", probs, values, preferred_element_type=jnp.float32
    ).reshape(pages_here, heads_here, head_dim)
    page_top = page_top.reshape(pages_here, heads_here)
    page_live = page_slot * page_len < owner_len
    member = (owner[:, None] == jnp.arange(total_req, dtype=jnp.int32)[None, :]) & page_live[
        :, None
    ]
    local_max = jnp.max(jnp.where(member[:, :, None], page_top[:, None, :], NEG_FILL), axis=0)
    member_t = member.astype(jnp.float32).T
    weight = jnp.exp(page_top - local_max[owner])
    sums = jnp.dot(member_t, weight * page_sum, precision=lax.Precision.HIGHEST)
    accs = jnp.dot(
        member_t,
        (weight[:, :, None] * page_acc).reshape(pages_here, -1),
        precision=lax.Precision.HIGHEST,
    )
    sums, accs = (sums, accs)
    merged = merged_2((local_max, sums, accs), "pg", merge_pair)
    start = lax.axis_index("pg") * own_req
    own_sum = lax.dynamic_slice_in_dim(merged[1], start, own_req, 0)
    own_acc = lax.dynamic_slice_in_dim(merged[2], start, own_req, 0)
    attn_dec = (own_acc.reshape(own_req, heads_here, head_dim) / own_sum[:, :, None]).reshape(
        own_req, -1
    )
    attn_dec = attn_dec.astype(jnp.bfloat16)
    attn_rows = jnp.concatenate([attn_dec, prefill_attn], axis=0)
    projected = jnp.dot(attn_rows, out_weight, preferred_element_type=jnp.float32)
    mixed_in = lax.psum_scatter(
        projected.astype(jnp.bfloat16), "kv", scatter_dimension=1, tiled=True
    ).astype(jnp.float32)
    middle = residual_in.astype(jnp.float32) + mixed_in
    full_width = residual_in.shape[1] * lax.axis_size("kv")
    in_squares = lax.psum(jnp.sum(middle * middle, axis=1), "kv")
    normed = (middle * lax.rsqrt(in_squares / full_width + EPSILON)[:, None] * norm_gain_in).astype(
        jnp.bfloat16
    )
    token_rows, top = expert_ids.shape
    copies = slot_table.shape[1]
    experts_total = slot_table.shape[0]
    kv_count = lax.axis_size("kv")
    capacity = kv_count * max(
        1,
        (token_rows * top * 5 + 4 * experts_total * kv_count - 1) // (4 * experts_total * kv_count),
    )
    slots_here = w_gate_up.shape[0]
    groups = lax.axis_size("pg")
    all_slots = slots_here * groups
    feature_cols = normed.shape[1]
    row_ids = lax.axis_index("pg") * token_rows + jnp.arange(token_rows, dtype=jnp.int32)
    parity = (row_ids[:, None] + jnp.arange(top, dtype=jnp.int32)[None, :]) % copies
    route_key = (expert_ids * copies + parity).reshape(-1)
    table_flat = slot_table.reshape(-1)
    table_index = jnp.arange(table_flat.shape[0], dtype=jnp.int32)
    target_slot = jnp.sum(
        jnp.where(route_key[:, None] == table_index[None, :], table_flat[None, :], 0), axis=1
    )
    match_count = (target_slot[:, None] == jnp.arange(all_slots, dtype=jnp.int32)[None, :]).astype(
        jnp.int32
    )
    rank = jnp.sum((jnp.cumsum(match_count, axis=0) - match_count) * match_count, axis=1)
    dest = target_slot * capacity + rank
    source_row = jnp.arange(token_rows * top, dtype=jnp.int32) // top
    outgoing = (
        jnp.zeros((all_slots * capacity, feature_cols), jnp.bfloat16)
        .at[dest]
        .set(normed[source_row])
    )
    outgoing = outgoing.reshape(groups, slots_here, capacity, feature_cols)
    arrived = lax.all_to_all(outgoing, "pg", split_axis=0, concat_axis=0, tiled=True)
    widened = lax.all_to_all(arrived, "kv", split_axis=2, concat_axis=3, tiled=True)
    gate_up = jnp.einsum(
        "pscd,sdf->pscf", widened, full_gate_up, preferred_element_type=jnp.float32
    )
    half = gate_up.shape[3] // 2
    hidden = (jax.nn.silu(gate_up[..., :half]) * gate_up[..., half:]).astype(jnp.bfloat16)
    produced = jnp.einsum(
        "pscf,sfd->pscd", hidden, full_down, preferred_element_type=jnp.float32
    ).astype(jnp.bfloat16)
    narrowed = lax.all_to_all(produced, "kv", split_axis=3, concat_axis=2, tiled=True)
    returned = lax.all_to_all(narrowed, "pg", split_axis=0, concat_axis=0, tiled=True)
    returned = returned.reshape(all_slots * capacity, feature_cols)
    picked = returned[dest].astype(jnp.float32).reshape(token_rows, top, feature_cols)
    mixed = middle + jnp.sum(picked * route_weight[:, :, None], axis=1)
    out_squares = lax.psum(jnp.sum(mixed * mixed, axis=1), "kv")
    return (mixed * lax.rsqrt(out_squares / full_width + EPSILON)[:, None] * norm_gain_out).astype(
        jnp.bfloat16
    )


def solution(mesh):
    in_specs = (
        P("pg", "kv"),
        P("pg", "kv"),
        P("pg", "kv"),
        P("pg", "kv", None, None),
        P(),
        P(),
        P("kv", None),
        P("kv"),
        P("kv"),
        P("pg", None),
        P("pg", None),
        P(),
        P("pg", "kv", None),
        P("pg", None, "kv"),
    )
    out_specs = P("pg", "kv")
    return jax.shard_map(local, mesh=mesh, in_specs=in_specs, out_specs=out_specs, check_vma=False)
```

profile of v0, /device:TPU:1, one launch (start us, length us, event | category | flops | bytes accessed | tf_op | source)
XLA Modules:
  0.0 587.1 jit_solution(4074204620895772323)
XLA Ops:
  7.8 1.3 gather_fusion
  9.2 81.1 %all-gather.3 = bf16[64,4,192]{2,1,0:T(4,128)(2,1)S(1)} all-gather(bf16[1,4,192]{2,1,0:T(4,128)(2,1)} %bitcast.147), channel_id=1, replica_groups=mesh['kv'=8,'pg'=64] {'pg'}, dimensions={0}, use_global_device_ids=true | all-gather | bytes 99840 | tf_op jit(solution)/shard_map/all_gather | solution.py:74
  91.0 1.5 fusion.47
  93.5 1.4 convolution_multiply_fusion
  96.4 73.7 %all-gather.1 = bf16[16384,3]{0,1:T(4,128)(2,1)S(1)} all-gather(bf16[256,3]{0,1:T(4,128)(2,1)S(1)} %convolution_convert_fusion.3), channel_id=3, replica_groups=mesh['kv'=8,'pg'=64] {'pg'}, dimensions={0}, use_global_device_ids=true | all-gather | bytes 99840 | tf_op jit(solution)/shard_map/all_gather | solution.py:12
  170.1 75.0 %all-gather = bf16[16384,3]{0,1:T(4,128)(2,1)S(1)} all-gather(bf16[256,3]{0,1:T(4,128)(2,1)S(1)} %convert_element_type.135), channel_id=2, replica_groups=mesh['kv'=8,'pg'=64] {'pg'}, dimensions={0}, use_global_device_ids=true | all-gather | bytes 99840 | tf_op jit(solution)/shard_map/all_gather | solution.py:12
  245.2 21.6 %all-gather.12.cloned.1.call-done = bf16[16384,192]{0,1:T(8,128)(2,1)} async-done(((bf16[256,192]{0,1:T(8,128)(2,1)}), bf16[16384,192]{0,1:T(8,128)(2,1)}) %all-gather.12.cloned.1.call-update) | async-done | bytes 6291472 | tf_op jit(solution)/shard_map/all_gather | solution.py:12
  266.7 6.3 %copy.134 = bf16[24,64,8,256]{3,2,0,1:T(8,128)(2,1)} copy(bf16[24,64,8,256]{3,2,1,0:T(8,128)(2,1)} %bitcast.131) | data formatting | bytes 12582912 | tf_op jit(solution)/shard_map/all_gather | solution.py:12
  274.0 64.9 %while.19 = (s32[]{:T(128)}, f32[256,3]{0,1:T(4,128)S(1)}, f32[256,3]{0,1:T(4,128)S(1)}, f32[256,192]{0,1:T(8,128)S(1)}, bf16[64,256,3]{1,2,0:T(4,128)(2,1)S(1)}...) while((s32[]{:T(128)}, f32[256,3]{0,1:T(4,128)S(1)}, ...), condition=%wide.region_5.6_spmd, body=%wide.region_4.5_spmd.sunk | while | flops 202757 | bytes 519319 | solution.py:24
  274.0 1.0 fusion.55
  275.0 1.0 fusion.55
  276.1 1.0 fusion.55
  277.1 1.0 fusion.55
  278.1 1.0 fusion.55
  279.2 1.0 fusion.55
  280.2 1.0 fusion.55
  281.2 1.0 fusion.55
  282.3 1.0 fusion.55
  283.3 1.0 fusion.55
  284.3 1.0 fusion.55
  285.3 1.0 fusion.55
  286.4 1.0 fusion.55
  287.4 1.0 fusion.55
  288.4 1.0 fusion.55
  289.5 1.0 fusion.55
  290.5 1.0 fusion.55
  291.5 1.0 fusion.55
  292.6 1.0 fusion.55
  293.6 1.0 fusion.55
  294.6 1.0 fusion.55
  295.6 1.0 fusion.55
  296.7 1.0 fusion.55
  297.7 1.0 fusion.55
  298.7 1.0 fusion.55
  299.8 1.0 fusion.55
  300.8 1.0 fusion.55
  301.8 1.0 fusion.55
  302.9 1.0 fusion.55
  303.9 1.0 fusion.55
  304.9 1.0 fusion.55
  305.9 1.0 fusion.55
  307.0 1.0 fusion.55
  308.0 1.0 fusion.55
  309.0 1.0 fusion.55
  310.1 1.0 fusion.55
  311.1 1.0 fusion.55
  312.1 1.0 fusion.55
  313.2 1.0 fusion.55
  314.2 1.0 fusion.55
  315.2 1.0 fusion.55
  342.4 1.2 reduce-window.6
  344.1 79.8 %reduce-scatter.4.cloned.1.call-done = bf16[192,64]{1,0:T(8,128)(2,1)} async-done(((bf16[1536,64]{1,0:T(8,128)(2,1)}), bf16[192,64]{1,0:T(8,128)(2,1)}) %reduce-scatter.4.cloned.1.call-update) | async-done | bytes 24592
  424.9 14.0 %psum.14 = f32[64]{0:T(128)S(1)} all-reduce(f32[64]{0:T(128)S(1)} %multiply_reduce_fusion.1), channel_id=1, replica_groups=mesh['kv'=8,'pg'=64] {'kv'}, use_global_device_ids=true, to_apply=%region_12.13 | all-reduce | flops 64 | bytes 512 | tf_op jit(solution)/shard_map/psum | solution.py:129
  439.1 3.9 scatter_custom_fusion
  443.0 44.3 %all_to_all.43 = bf16[64,1,16,192]{3,2,1,0:T(8,128)(2,1)S(1)} all-to-all(bf16[64,1,16,192]{3,2,1,0:T(8,128)(2,1)S(1)} %bitcast.134), channel_id=1, replica_groups=mesh['kv'=8,'pg'=64] {'pg'}, dimensions={0} | all-to-all | bytes 786432 | tf_op jit(solution)/shard_map/all_to_all | solution.py:165
  487.4 15.2 %all_to_all.44 = bf16[64,1,16,192]{3,0,1,2:T(8,128)(2,1)S(1)} all-to-all(bf16[64,1,16,192]{3,0,1,2:T(8,128)(2,1)S(1)} %copy.117), channel_id=1, replica_groups=mesh['kv'=8,'pg'=64] {'kv'}, dimensions={2} | all-to-all | bytes 786432 | tf_op jit(solution)/shard_map/all_to_all | solution.py:166
  503.4 2.5 fusion.7
  505.9 2.1 fusion.5
  509.1 11.5 %all_to_all.45 = bf16[8,2,12288]{2,1,0:T(2,128)(2,1)S(1)} all-to-all(bf16[8,2,12288]{2,1,0:T(2,128)(2,1)S(1)} %reshape.463), channel_id=1, replica_groups=mesh['kv'=8,'pg'=64] {'kv'}, dimensions={0} | all-to-all | bytes 786432 | tf_op jit(solution)/shard_map/all_to_all | solution.py:175
  522.0 1.1 copy.123
  523.1 10.2 %all-to-all-start.3 = ((bf16[64,1,16,192]{3,2,1,0:T(8,128)(2,1)}), bf16[64,1,16,192]{3,2,1,0:T(8,128)(2,1)S(1)}, u32[]{:S(2)}, u32[]{:S(2)}) async-start(bf16[64,1,16,192]{3,2,1,0:T(8,128)(2,1)} %copy.123), calls=%async_computation.3 | async-start | bytes 1048576 | tf_op jit(solution)/shard_map/all_to_all | solution.py:176
  533.4 29.0 %all-to-all-done.3 = bf16[64,1,16,192]{3,2,1,0:T(8,128)(2,1)S(1)} async-done(((bf16[64,1,16,192]{3,2,1,0:T(8,128)(2,1)}), bf16[64,1,16,192]{3,2,1,0:T(8,128)(2,1)S(1)}, u32[]{:S(2)}, u32[]{:S(2)}) %all-to-all-start.3) | async-done | bytes 393248 | tf_op jit(solution)/shard_map/all_to_all | solution.py:176
  562.3 1.9 gather_fusion.3
  564.6 15.2 %psum.15 = f32[64]{0:T(128)S(1)} all-reduce(f32[64]{0:T(128)S(1)} %multiply_reduce_fusion), channel_id=1, replica_groups=mesh['kv'=8,'pg'=64] {'kv'}, use_global_device_ids=true, to_apply=%region_16.17 | all-reduce | flops 64 | bytes 512 | tf_op jit(solution)/shard_map/psum | solution.py:180
  (179 shorter events, 38.3 us)
Async XLA Ops:
  6.5 332.8 %copy-start = (bf16[192,1536]{1,0:T(8,128)(2,1)S(1)}, bf16[192,1536]{1,0:T(8,128)(2,1)}, u32[]{:S(2)}) copy-start(bf16[192,1536]{1,0:T(8,128)(2,1)} %param.22) | copy-start | bytes 1769476
  6.5 260.2 %all-gather.12.cloned.1.call-start = ((), (), s32[]{:S(2)}) async-start(), calls=%async_computation.7 | async-start | bytes 6389760 | tf_op jit(solution)/shard_map/all_gather | solution.py:12
  96.0 327.9 %reduce-scatter.4.cloned.1.call-start = ((), (), s32[]{:S(2)}) async-start(), calls=%async_computation.8 | async-start | bytes 442368
  273.0 66.3 %copy-start.2 = (bf16[60,192]{1,0:T(8,128)(2,1)S(1)}, bf16[60,192]{1,0:T(8,128)(2,1)}, u32[]{:S(2)}) copy-start(bf16[60,192]{1,0:T(8,128)(2,1)} %param.18) | copy-start | bytes 69124
  273.0 68.9 %copy-start.4 = (s32[64,8]{0,1:T(8,128)S(1)}, s32[64,8]{0,1:T(8,128)}, u32[]{:S(2)}) copy-start(s32[64,8]{0,1:T(8,128)} %param.25) | copy-start | bytes 6148
  273.0 69.1 %copy-start.7 = (s32[40,2]{0,1:T(2,128)S(1)}, s32[40,2]{0,1:T(2,128)}, u32[]{:S(2)}) copy-start(s32[40,2]{0,1:T(2,128)} %param.27) | copy-start | bytes 964
  273.9 150.9 %copy-start.1 = (bf16[64,192]{1,0:T(8,128)(2,1)S(1)}, bf16[64,192]{1,0:T(8,128)(2,1)}, u32[]{:S(2)}) copy-start(bf16[64,192]{1,0:T(8,128)(2,1)} %param.16) | copy-start | bytes 73732
  274.0 165.0 %copy-start.5 = (f32[192]{0:T(256)S(1)}, f32[192]{0:T(256)}, u32[]{:S(2)}) copy-start(f32[192]{0:T(256)} %param.23) | copy-start | bytes 2308
  340.6 162.8 %all-gather.8.cloned.1.call-start = ((), (), s32[]{:S(2)}) async-start(), calls=%async_computation.5 | async-start | bytes 3538944 | tf_op jit(solution)/shard_map/all_gather | solution.py:71
  341.3 164.6 %all-gather.10.cloned.1.call-start = ((), (), s32[]{:S(2)}) async-start(), calls=%async_computation.6 | async-start | bytes 1769472 | tf_op jit(solution)/shard_map/all_gather | solution.py:72
  509.1 24.2 %copy-start.3 = (f32[64,8]{0,1:T(8,128)S(1)}, f32[64,8]{0,1:T(8,128)}, u32[]{:S(2)}) copy-start(f32[64,8]{0,1:T(8,128)} %param.26) | copy-start | bytes 6148
  521.8 58.0 %copy-start.6 = (f32[192]{0:T(256)S(1)}, f32[192]{0:T(256)}, u32[]{:S(2)}) copy-start(f32[192]{0:T(256)} %param.24) | copy-start | bytes 2308
  523.1 39.3 %all-to-all-start.3 = ((bf16[64,1,16,192]{3,2,1,0:T(8,128)(2,1)}), bf16[64,1,16,192]{3,2,1,0:T(8,128)(2,1)S(1)}, u32[]{:S(2)}, u32[]{:S(2)}) async-start(bf16[64,1,16,192]{3,2,1,0:T(8,128)(2,1)} %copy.123), calls=%async_computation.3 | async-start | bytes 1048576 | tf_op jit(solution)/shard_map/all_to_all | solution.py:176
Sparse Core Ops, SparseCore 0:
  96.1 170.5 all-gather.11
  340.7 83.2 reduce-scatter.3
  426.3 36.3 all-gather.7
  464.9 32.2 all-gather.9
where the time goes:
time: 590 us; the launch traced here: 587 us
  blocking collectives  330 us (56%)
  waiting for transfers between devices  132 us (22%)
  other arithmetic  67.9 us (12%)
  local copies, waits for them, and re-layouts  23.6 us (4%)
  between operations  13.5 us (2%)
  starting transfers between devices  10.3 us (2%)
  matrix products  8.78 us (1%)
    all_gather x2, blocking collectives, merged_2(): lax.all_gather(a.astype(kind), axis)  149 us
    unnamed x5, waiting for transfers between devices  81.1 us
    all_gather x1, blocking collectives, local(): gathered = lax.all_gather(queries, 'pg', axis=0, tiled=True)  81.1 us
    add x63, other arithmetic, merge_pair(): acc_a + acc_b  61.7 us
    all_to_all x1, blocking collectives, local(): lax.all_to_all(outgoing, 'pg', split_axis=0, concat_axis=0, tiled=True)  44.3 us
    all_to_all x1, waiting for transfers between devices, local(): lax.all_to_all(narrowed, 'pg', split_axis=0, concat_axis=0, tiled=True)  29 us
    all_gather x1, waiting for transfers between devices, merged_2(): lax.all_gather(a.astype(kind), axis)  21.6 us
    psum x1, blocking collectives, local(): out_squares = lax.psum(jnp.sum(mixed * mixed, axis=1), 'kv')  15.2 us
  transfers between devices with their start and end apart: 5, of which 3 were waited for; matrix products, arithmetic and copies ran while one was open for 2% of the time, Pallas kernels for 0%

commit v1 on v0

v1 whole, which is shorter than its diff:
```python
import functools
import jax
import jax.numpy as jnp
from jax import lax
from jax.experimental import pallas as pl
from jax.experimental.pallas import tpu as pltpu
from jax.sharding import PartitionSpec as P

NEG_FILL = -1e30
EPSILON = 1e-06
OFFSET = 4096.0
MESH = pl.DeviceIdType.MESH
NY = 4
F32 = jnp.float32
BF16 = jnp.bfloat16


def iota(shape, dim):
    return lax.broadcasted_iota(jnp.int32, shape, dim)


def remote(src, dst, ssem, rsem, dev):
    return pltpu.make_async_remote_copy(
        src_ref=src,
        dst_ref=dst,
        send_sem=ssem,
        recv_sem=rsem,
        device_id=dev,
        device_id_type=MESH,
    )


def greet(ny, nz, nkv, yy, zz, kk):
    barrier = pltpu.get_barrier_semaphore()

    def z_body(d, c):
        peer = yy * nz + lax.rem(zz + d, nz)
        pl.semaphore_signal(barrier, inc=1, device_id={"pg": peer}, device_id_type=MESH)
        return c

    lax.fori_loop(1, nz, z_body, 0)
    for d in range(1, ny):
        peer = lax.rem(yy + d, ny) * nz + zz
        pl.semaphore_signal(barrier, inc=1, device_id={"pg": peer}, device_id_type=MESH)
    for d in range(1, nkv):
        peer = lax.rem(kk + d, nkv)
        pl.semaphore_signal(barrier, inc=1, device_id={"kv": peer}, device_id_type=MESH)
    pl.semaphore_wait(barrier, nz - 1 + ny - 1 + nkv - 1)


def to_tiles(rows, data):
    out = []
    for j in range(len(data) // 2):
        even, odd = data[2 * j], data[2 * j + 1]
        out.append(even[:, :128])
        out.append(even[:, 128:] + odd[:, :128])
        out.append(odd[:, 128:])
    return jnp.concatenate(out, axis=1)


def placement(parity, transposed=False):
    shape = (256, 192) if transposed else (192, 256)
    narrow, wide = (1, 0) if transposed else (0, 1)
    return (iota(shape, wide) == iota(shape, narrow) + 64 * parity).astype(BF16)


def stat_tile(x2):
    n = x2.shape[0]
    lane = iota((128, 256), 0) - 64
    head = iota((128, 256), 1) // 64
    pick = ((lane >= 0) & (lane < 9) & (lane % 3 == head) & (head < 3)).astype(BF16)
    spread = jnp.dot(x2, pick, preferred_element_type=F32)
    low = pltpu.roll(spread[:, :128], n - 4, 0)
    return jnp.where(iota((n, 128), 0) % 8 < 4, low, spread[:, 128:])


def split3(x):
    hi = x.astype(BF16).astype(F32)
    mid = (x - hi).astype(BF16).astype(F32)
    return hi, mid, x - hi - mid


def encode(acc, lse):
    n = acc.shape[0]
    sub, lane = iota((n, 128), 0) % 8, iota((n, 128), 1)
    down = pltpu.roll(lse, 4, 0)
    first = pltpu.roll(down, 64, 1)
    third = pltpu.roll(lse, 64, 1)
    which = (lane - 64) % 3
    value = jnp.where(which == 0, first, jnp.where(which == 1, down, third))
    hi, mid, lo = split3(value)
    part = (lane - 64) // 3
    stat = jnp.where(part == 0, hi, jnp.where(part == 1, mid, lo))
    is_stat = (sub >= 4) & (lane >= 64)
    return jnp.where(is_stat, jnp.where(lane < 73, stat, 0.0), acc).astype(BF16)


def merge(x):
    n, m, _ = x.shape
    flat = x.reshape(n * m, 128)
    lse = stat_tile(flat).reshape(n, m, 128)
    acc = flat.astype(F32).reshape(n, m, 128)
    top = jnp.max(lse, axis=0)
    weight = jnp.exp(lse - top[None])
    total = jnp.sum(weight, axis=0)
    return jnp.sum(weight * acc, axis=0) / total, top + jnp.log(total)


def attention_kernel(
    nz,
    nkv,
    q_ref,
    kv_ref,
    pt_ref,
    le_ref,
    pre_ref,
    w_ref,
    res_ref,
    gi_ref,
    go_ref,
    ids_ref,
    rw_ref,
    st_ref,
    wgu_ref,
    wd_ref,
    blk_ref,
    mid_ref,
    gout_ref,
    wgu_all,
    wd_all,
    qtile,
    qall,
    part,
    ybuf,
    zsend,
    zbuf,
    pre_s,
    proj,
    rsbuf,
    ressend,
    resbuf,
    gsend,
    gbuf,
    wds,
    s_q,
    r_q,
    s_qy,
    r_qy,
    s_py,
    r_py,
    s_pz,
    r_pz,
    s_rs,
    r_rs,
    s_res,
    r_res,
    s_g,
    r_g,
    s_wg,
    r_wg,
    s_wd,
    r_wd,
    l_w,
):
    ny = NY
    nx = nkv // 2
    pg, kk = lax.axis_index("pg"), lax.axis_index("kv")
    yy, zz = pg // nz, lax.rem(pg, nz)
    xx, cc = kk // 2, lax.rem(kk, 2)
    pages = kv_ref.shape[0]
    rows = pages * 8
    width = w_ref.shape[1]
    tops = ids_ref.shape[1]
    own_req = q_ref.shape[0]

    greet(ny, nz, nkv, yy, zz, kk)

    def z_peer(d):
        return lax.rem(zz + d, nz)

    def y_peer(d):
        return lax.rem(yy + d, ny)

    def k_peer(d):
        return lax.rem(kk + d, nkv)

    q32 = q_ref[...].astype(F32)
    qtile[...] = jnp.zeros_like(qtile)
    qtile[0:own_req, :] = q32[:, :128]
    qtile[4 : 4 + own_req, 0:64] = q32[:, 128:]
    qall[yy, zz] = qtile[...].astype(BF16)

    def q_copy(src_z, dst_z):
        return remote(
            qall.at[yy, src_z],
            qall.at[yy, src_z],
            s_q.at[dst_z],
            r_q.at[src_z],
            {"pg": yy * nz + dst_z},
        )

    def q_start(d, c):
        q_copy(zz, z_peer(d)).start()
        return c

    lax.fori_loop(1, nz, q_start, 0)

    def wg_copy(src_x, dst_x):
        return remote(
            wgu_ref.at[0],
            wgu_all.at[src_x],
            s_wg.at[dst_x],
            r_wg.at[src_x],
            {"kv": dst_x * 2 + cc},
        )

    def wd_copy(src_x, dst_x):
        return remote(
            wds, wd_all.at[src_x], s_wd.at[dst_x], r_wd.at[src_x], {"kv": dst_x * 2 + cc}
        )

    for d in range(1, nx):
        wg_copy(xx, lax.rem(xx + d, nx)).start()
    own_wg = pltpu.make_async_copy(wgu_ref.at[0], wgu_all.at[xx], l_w.at[0])
    own_wg.start()
    spread = placement(cc)
    wds[...] = jnp.dot(wd_ref[0], spread, preferred_element_type=F32).astype(BF16)
    for d in range(1, nx):
        wd_copy(xx, lax.rem(xx + d, nx)).start()
    own_wd = pltpu.make_async_copy(wds, wd_all.at[xx], l_w.at[1])
    own_wd.start()

    ressend[...] = (
        jnp.dot(res_ref[...], spread, preferred_element_type=F32)
        .astype(BF16)
        .reshape(ressend.shape)
    )
    gsend[...] = jnp.zeros_like(gsend)
    gsend[0:1, 0:192] = gi_ref[...]
    gsend[1:2, 0:192] = go_ref[...]
    gains = gsend[...]
    gsend[...] = jnp.where(cc == 1, pltpu.roll(gains, 64, 1), gains)

    def res_copy(src_k, dst_k):
        return remote(
            ressend.at[dst_k], resbuf.at[src_k], s_res.at[dst_k], r_res.at[src_k], {"kv": dst_k}
        )

    def g_copy(src_k, dst_k):
        return remote(gsend, gbuf.at[src_k], s_g.at[dst_k], r_g.at[src_k], {"kv": dst_k})

    for d in range(1, nkv):
        res_copy(kk, k_peer(d)).start()
        g_copy(kk, k_peer(d)).start()
    resbuf[kk] = ressend[kk]
    gbuf[kk] = gsend[...]

    pre_s[0:own_req, :] = jnp.zeros((own_req, pre_s.shape[1]), F32)
    pre_s[own_req:, :] = pre_ref[...].astype(F32)
    done = jnp.dot(pre_s[...].astype(BF16), w_ref[...], preferred_element_type=F32)
    proj[...] = done.astype(BF16).reshape(proj.shape)
    head_rows = done[0:8]

    def rs_copy(src_k, dst_k):
        return remote(
            proj.at[dst_k], rsbuf.at[src_k], s_rs.at[dst_k], r_rs.at[src_k], {"kv": dst_k}
        )

    for k in range(1, nkv):

        @pl.when(kk != k)
        def _():
            rs_copy(kk, k).start()

    page_row = iota((rows, 1), 0) // 8
    head = iota((rows, 1), 0) % 8
    mine = pt_ref[...] == page_row + pg * pages
    place = iota(mine.shape, 1).astype(F32)
    entry = jnp.sum(jnp.where(mine, place, 0.0), axis=1, keepdims=True)
    cached = jnp.sum(jnp.where(mine, le_ref[...], 0.0), axis=1, keepdims=True)
    owner = jnp.floor(entry * 0.25)
    limit = cached - (entry - 4.0 * owner) * 128.0
    owner_pg = jnp.floor(owner * 0.25)
    owner_col = 8.0 * owner_pg + (owner - 4.0 * owner_pg)
    wanted = owner_col + jnp.where(head == 2, 4.0, 0.0)
    npg = ny * nz
    select = (iota((rows, npg * 8), 1).astype(F32) == wanted) & (head < 3)
    select = select.astype(BF16)

    def q_wait(d, c):
        q_copy(z_peer(d), zz).wait_recv()
        return c

    lax.fori_loop(1, nz, q_wait, 0)

    def qy_copy(src_y, dst_y):
        return remote(
            qall.at[src_y], qall.at[src_y], s_qy.at[dst_y], r_qy.at[src_y], {"pg": dst_y * nz + zz}
        )

    for d in range(1, ny):
        qy_copy(yy, y_peer(d)).start()
    for d in range(1, ny):
        qy_copy(y_peer(d), yy).wait_recv()

    lane = iota((rows, 128), 1)
    queries = jnp.dot(select, qall[...].reshape(npg * 8, 128), preferred_element_type=F32)
    queries = jnp.where(head == 1, pltpu.roll(queries, 64, 1), queries)
    queries = jnp.where(lane < 64, queries, 0.0)
    scores = jnp.concatenate(
        [
            lax.dot_general(
                queries[8 * i : 8 * i + 8].astype(BF16),
                kv_ref[i],
                (((1,), (1,)), ((), ())),
                preferred_element_type=F32,
            )
            for i in range(pages)
        ],
        axis=0,
    ) * (64**-0.5)
    live = lane.astype(F32) < limit
    masked = jnp.where(live, scores, NEG_FILL)
    top = jnp.max(masked, axis=1, keepdims=True)
    probs = jnp.where(live, jnp.exp(masked - top), 0.0).astype(BF16).astype(F32)
    total = jnp.sum(probs, axis=1, keepdims=True)
    acc = jnp.concatenate(
        [
            jnp.dot(probs[8 * i : 8 * i + 8].astype(BF16), kv_ref[i], preferred_element_type=F32)
            for i in range(pages)
        ],
        axis=0,
    )
    alive = limit > 0.0
    lse = jnp.where(alive, top + jnp.log(jnp.maximum(total, 1e-30)), NEG_FILL)
    acc = acc / jnp.where(alive, total, 1.0)

    eye = iota((rows, rows), 0) == iota((rows, rows), 1)
    owner_row = jnp.sum(jnp.where(eye, owner, 0.0), axis=0, keepdims=True)
    lse_row = jnp.sum(jnp.where(eye, lse, 0.0), axis=0, keepdims=True)
    head_row = iota((1, rows), 1) % 8
    group = (owner == owner_row) & (head == head_row) & (lse_row > -1e29)
    peak = jnp.max(jnp.where(group, lse_row, NEG_FILL), axis=1, keepdims=True)
    mass = jnp.sum(jnp.where(group, jnp.exp(lse_row - peak), 0.0), axis=1, keepdims=True)
    joint = peak + jnp.log(jnp.maximum(mass, 1e-30))
    acc = acc * jnp.where(alive, jnp.exp(lse - joint), 0.0)
    earlier = jnp.sum(
        jnp.where(group & (iota((rows, rows), 1) < iota((rows, rows), 0)), 1.0, 0.0),
        axis=1,
        keepdims=True,
    )
    code = jnp.where(alive & (earlier == 0.0), joint + OFFSET, 0.0)
    hi, mid, lo = split3(code)
    stats = jnp.where(
        lane == 64 + head,
        hi,
        jnp.where(lane == 67 + head, mid, jnp.where(lane == 70 + head, lo, 0.0)),
    )
    stats = jnp.where(head < 3, stats, 0.0)
    stats = pltpu.roll(stats, 3, 0) + pltpu.roll(stats, 2, 0) + pltpu.roll(stats, 1, 0)
    turned = pltpu.roll(acc, 64, 1)
    placed = jnp.where(
        head == 1,
        jnp.where(lane >= 64, acc, 0.0),
        jnp.where(lane < 64, turned, 0.0),
    )
    placed = jnp.where(head == 3, stats, placed)
    placed_hi = placed.astype(BF16)
    placed_lo = (placed - placed_hi.astype(F32)).astype(BF16)
    out_row = iota((npg * 8, rows), 0)
    request = ((out_row // 8) * 4 + out_row % 4).astype(F32)
    half = (out_row // 4) % 2
    head_all = iota((npg * 8, rows), 1) % 8
    scatter = (request == owner_row) & (head_all // 2 == half)
    scattered = jnp.dot(
        scatter.astype(BF16),
        jnp.concatenate([placed_hi, placed_lo], axis=1),
        preferred_element_type=F32,
    )
    part[...] = (scattered[:, :128] + scattered[:, 128:]).astype(BF16).reshape(part.shape)

    def py_copy(src_y, dst_y):
        return remote(
            part.at[dst_y], ybuf.at[src_y], s_py.at[dst_y], r_py.at[src_y], {"pg": dst_y * nz + zz}
        )

    for d in range(1, ny):
        py_copy(yy, y_peer(d)).start()
    ybuf[yy] = part[yy]
    for d in range(1, ny):
        py_copy(y_peer(d), yy).wait_recv()
    acc_y, lse_y = merge(ybuf[...].reshape(ny, nz * 8, 128))
    zsend[...] = encode(acc_y, lse_y).reshape(zsend.shape)

    def pz_copy(src_z, dst_z):
        return remote(
            zsend.at[dst_z], zbuf.at[src_z], s_pz.at[dst_z], r_pz.at[src_z], {"pg": yy * nz + dst_z}
        )

    def pz_start(d, c):
        pz_copy(zz, z_peer(d)).start()
        return c

    lax.fori_loop(1, nz, pz_start, 0)
    zbuf[zz] = zsend[zz]

    def pz_wait(d, c):
        pz_copy(z_peer(d), zz).wait_recv()
        return c

    lax.fori_loop(1, nz, pz_wait, 0)
    attn, _ = merge(zbuf[...])
    attn = attn.astype(BF16).astype(F32)
    sub8, lane8 = iota((8, 128), 0), iota((8, 128), 1)
    pair = jnp.where(sub8 < 4, attn, 0.0).astype(BF16)
    last = jnp.where((sub8 < 4) & (lane8 < 64), pltpu.roll(attn, 4, 0), 0.0).astype(BF16)
    dec = jnp.dot(pair, w_ref[0:128, :], preferred_element_type=F32)
    dec = dec + jnp.dot(last[:, :64], w_ref[128:192, :], preferred_element_type=F32)
    proj[0] = (head_rows + dec).astype(BF16)

    @pl.when(kk != 0)
    def _():
        rs_copy(kk, 0).start()

    slot_lane = iota((st_ref.shape[0], 128), 1)
    expert = iota((st_ref.shape[0], 128), 0).astype(F32) + 1.0
    holder = [
        jnp.sum(jnp.where(st_ref[:, j : j + 1] == slot_lane, expert, 0.0), axis=0, keepdims=True)
        - 1.0
        for j in range(2)
    ]
    ids = ids_ref[pl.ds(pl.multiple_of(8 * kk, 8), 8), :].astype(F32)
    gate = rw_ref[pl.ds(pl.multiple_of(8 * kk, 8), 8), :]
    odd = iota((8, 1), 0) % 2 == 1
    dense = jnp.zeros((8, 128), F32)
    for j in range(tops):
        flip = odd if j % 2 == 0 else jnp.logical_not(odd)
        hit = ids[:, j : j + 1] == jnp.where(flip, holder[1], holder[0])
        dense = dense + jnp.where(hit, gate[:, j : j + 1], 0.0)
    dense_hi = dense.astype(BF16).astype(F32)
    dense_lo = pltpu.roll(dense - dense_hi, 64, 1)
    blk_ref[:, width:] = jnp.where(lane8 < 64, dense_hi, dense_lo).astype(BF16)

    for d in range(1, nkv):
        res_copy(k_peer(d), kk).wait_recv()
        g_copy(k_peer(d), kk).wait_recv()
    rsbuf[kk] = proj[kk]
    for d in range(1, nkv):
        rs_copy(k_peer(d), kk).wait_recv()
    gain = to_tiles(8, [gbuf[k] for k in range(nkv)])
    residual = to_tiles(8, [resbuf[k].astype(F32) for k in range(nkv)])
    projected = rsbuf[0].astype(F32)
    for k in range(1, nkv):
        projected = projected + rsbuf[k].astype(F32)
    middle = residual + projected
    square = jnp.sum(middle * middle, axis=1, keepdims=True) / width
    mid_ref[...] = middle
    gout_ref[...] = gain[1:2]
    blk_ref[:, :width] = (middle * lax.rsqrt(square + EPSILON) * gain[0:1]).astype(BF16)

    def z_sent(d, c):
        q_copy(zz, z_peer(d)).wait_send()
        pz_copy(zz, z_peer(d)).wait_send()
        return c

    lax.fori_loop(1, nz, z_sent, 0)
    for d in range(1, ny):
        qy_copy(yy, y_peer(d)).wait_send()
        py_copy(yy, y_peer(d)).wait_send()
    for d in range(1, nkv):
        res_copy(kk, k_peer(d)).wait_send()
        g_copy(kk, k_peer(d)).wait_send()
        rs_copy(kk, k_peer(d)).wait_send()
    own_wg.wait()
    own_wd.wait()
    for d in range(1, nx):
        peer = lax.rem(xx + d, nx)
        wg_copy(xx, peer).wait_send()
        wd_copy(xx, peer).wait_send()
        wg_copy(peer, xx).wait_recv()
        wd_copy(peer, xx).wait_recv()


def expert_kernel(
    nz,
    nkv,
    blk_ref,
    mid_ref,
    gout_ref,
    wgu_all,
    wd_all,
    out_ref,
    wgu,
    wdn,
    xbuf,
    obuf,
    ybuf,
    zsend,
    zbuf,
    fsend,
    fbuf,
    l_w,
    s_w,
    r_w,
    s_xz,
    r_xz,
    s_xy,
    r_xy,
    s_oy,
    r_oy,
    s_oz,
    r_oz,
    s_f,
    r_f,
):
    ny = NY
    pg, kk = lax.axis_index("pg"), lax.axis_index("kv")
    yy, zz = pg // nz, lax.rem(pg, nz)
    cc = lax.rem(kk, 2)
    sibling = kk + 1 - 2 * cc
    width = mid_ref.shape[1]

    greet(ny, nz, nkv, yy, zz, kk)

    def z_peer(d):
        return lax.rem(zz + d, nz)

    def y_peer(d):
        return lax.rem(yy + d, ny)

    def k_peer(d):
        return lax.rem(kk + d, nkv)

    xbuf[yy, zz] = blk_ref[...]

    def xz_copy(src_z, dst_z):
        return remote(
            xbuf.at[yy, src_z],
            xbuf.at[yy, src_z],
            s_xz.at[dst_z],
            r_xz.at[src_z],
            {"pg": yy * nz + dst_z},
        )

    def xz_start(d, c):
        xz_copy(zz, z_peer(d)).start()
        return c

    lax.fori_loop(1, nz, xz_start, 0)

    own_wg = pltpu.make_async_copy(wgu_all, wgu.at[:, cc], l_w.at[0])
    own_wd = pltpu.make_async_copy(wd_all, wdn.at[cc], l_w.at[1])
    own_wg.start()
    own_wd.start()

    def w_copies(core):
        return (
            remote(wgu_all, wgu.at[:, core], s_w.at[0], r_w.at[0], {"kv": sibling}),
            remote(wd_all, wdn.at[core], s_w.at[1], r_w.at[1], {"kv": sibling}),
        )

    for copy in w_copies(cc):
        copy.start()

    def xz_wait(d, c):
        xz_copy(z_peer(d), zz).wait_recv()
        return c

    lax.fori_loop(1, nz, xz_wait, 0)

    def xy_copy(src_y, dst_y):
        return remote(
            xbuf.at[src_y], xbuf.at[src_y], s_xy.at[dst_y], r_xy.at[src_y], {"pg": dst_y * nz + zz}
        )

    for d in range(1, ny):
        xy_copy(yy, y_peer(d)).start()
    own_wg.wait()
    own_wd.wait()
    for copy in w_copies(1 - cc):
        copy.wait_recv()

    def oy_copy(src_y, dst_y):
        return remote(
            obuf.at[dst_y], ybuf.at[src_y], s_oy.at[dst_y], r_oy.at[src_y], {"pg": dst_y * nz + zz}
        )

    def experts(y):
        x = xbuf[y].reshape(nz * 8, width + 128)
        gate_up = jnp.dot(
            x[:, :width], wgu[...].reshape(width, wgu.shape[3]), preferred_element_type=F32
        )
        ff = gate_up.shape[1] // 2
        v = gate_up[:, :ff]
        hidden = (v / (1.0 + jnp.exp(-v)) * gate_up[:, ff:]).astype(BF16)
        pieces = [
            jnp.dot(hidden, wdn[k % 2, k // 2], preferred_element_type=F32) for k in range(nkv)
        ]
        produced = to_tiles(nz * 8, pieces).astype(BF16).astype(F32)
        lane = iota((nz * 8, 128), 1)
        share = jnp.where(lane % 64 == pg, x[:, width:].astype(F32), 0.0)
        share = jnp.sum(share, axis=1, keepdims=True)
        obuf[y] = (produced * share).astype(BF16).reshape(nz, 8, width)

    for d in range(ny):
        if d > 0:
            xy_copy(y_peer(d), yy).wait_recv()
        experts(y_peer(d))
        if d > 0:
            oy_copy(yy, y_peer(d)).start()
    ybuf[yy] = obuf[yy]
    for d in range(1, ny):
        oy_copy(y_peer(d), yy).wait_recv()

    def add_y(z, c):
        total = ybuf[0, z].astype(F32)
        for y in range(1, ny):
            total = total + ybuf[y, z].astype(F32)
        zsend[z] = total.astype(BF16)
        return c

    lax.fori_loop(0, nz, add_y, 0)

    def oz_copy(src_z, dst_z):
        return remote(
            zsend.at[dst_z], zbuf.at[src_z], s_oz.at[dst_z], r_oz.at[src_z], {"pg": yy * nz + dst_z}
        )

    def oz_start(d, c):
        oz_copy(zz, z_peer(d)).start()
        return c

    lax.fori_loop(1, nz, oz_start, 0)
    zbuf[zz] = zsend[zz]

    def oz_wait(d, c):
        oz_copy(z_peer(d), zz).wait_recv()
        return c

    lax.fori_loop(1, nz, oz_wait, 0)
    mixed = mid_ref[...]
    for z in range(nz):
        mixed = mixed + zbuf[z].astype(F32)
    square = jnp.sum(mixed * mixed, axis=1, keepdims=True) / width
    fsend[...] = (mixed * lax.rsqrt(square + EPSILON) * gout_ref[...]).astype(BF16)

    def f_copy(src_k, dst_k):
        start = pl.multiple_of(128 * (3 * (dst_k // 2) + lax.rem(dst_k, 2)), 128)
        return remote(
            fsend.at[:, pl.ds(start, 256)],
            fbuf.at[src_k],
            s_f.at[dst_k],
            r_f.at[src_k],
            {"kv": dst_k},
        )

    for d in range(1, nkv):
        f_copy(kk, k_peer(d)).start()
    fbuf[kk] = fsend[:, pl.ds(pl.multiple_of(128 * (3 * (kk // 2) + cc), 128), 256)]
    for d in range(1, nkv):
        f_copy(k_peer(d), kk).wait_recv()
    out_ref[...] = jnp.dot(
        fbuf[...].reshape(nkv * 8, 256), placement(cc, True), preferred_element_type=F32
    ).astype(BF16)

    def z_sent(d, c):
        xz_copy(zz, z_peer(d)).wait_send()
        oz_copy(zz, z_peer(d)).wait_send()
        return c

    lax.fori_loop(1, nz, z_sent, 0)
    for d in range(1, ny):
        xy_copy(yy, y_peer(d)).wait_send()
        oy_copy(yy, y_peer(d)).wait_send()
    for d in range(1, nkv):
        f_copy(kk, k_peer(d)).wait_send()
    for copy in w_copies(cc):
        copy.wait_send()


def dma(n):
    return pltpu.SemaphoreType.DMA((n,))


def local(
    npg,
    nkv,
    residual_in,
    queries,
    prefill_attn,
    kv_cache,
    page_table,
    lengths,
    out_weight,
    norm_gain_in,
    norm_gain_out,
    expert_ids,
    route_weight,
    slot_table,
    w_gate_up,
    w_down,
):
    nz, nx, ny = npg // NY, nkv // 2, NY
    width = out_weight.shape[1]
    ff2, ff = w_gate_up.shape[2], w_down.shape[1]
    pages = kv_cache.shape[0]
    entries = page_table.size
    vmem, hbm = pl.BlockSpec(memory_space=pltpu.VMEM), pl.BlockSpec(memory_space=pl.ANY)
    block, middle, gain_out, wgu_all, wd_all = pl.pallas_call(
        functools.partial(attention_kernel, nz, nkv),
        out_shape=(
            jax.ShapeDtypeStruct((8, width + 128), BF16),
            jax.ShapeDtypeStruct((8, width), F32),
            jax.ShapeDtypeStruct((1, width), F32),
            jax.ShapeDtypeStruct((nx, 192, ff2), BF16),
            jax.ShapeDtypeStruct((nx, ff, 256), BF16),
        ),
        in_specs=[vmem] * 12 + [hbm, vmem],
        out_specs=(vmem, vmem, vmem, hbm, hbm),
        scratch_shapes=[
            pltpu.VMEM((8, 128), F32),
            pltpu.VMEM((ny, nz, 8, 128), BF16),
            pltpu.VMEM((ny, nz, 8, 128), BF16),
            pltpu.VMEM((ny, nz, 8, 128), BF16),
            pltpu.VMEM((nz, 8, 128), BF16),
            pltpu.VMEM((nz, 8, 128), BF16),
            pltpu.VMEM((64, 192), F32),
            pltpu.VMEM((nkv, 64 // nkv, width), BF16),
            pltpu.VMEM((nkv, 64 // nkv, width), BF16),
            pltpu.VMEM((nkv, 64 // nkv, 256), BF16),
            pltpu.VMEM((nkv, 64 // nkv, 256), BF16),
            pltpu.VMEM((8, 256), F32),
            pltpu.VMEM((nkv, 8, 256), F32),
            pltpu.VMEM((ff, 256), BF16),
            dma(nz),
            dma(nz),
            dma(ny),
            dma(ny),
            dma(ny),
            dma(ny),
            dma(nz),
            dma(nz),
            dma(nkv),
            dma(nkv),
            dma(nkv),
            dma(nkv),
            dma(nkv),
            dma(nkv),
            dma(nx),
            dma(nx),
            dma(nx),
            dma(nx),
            dma(2),
        ],
        compiler_params=pltpu.CompilerParams(
            collective_id=0, has_side_effects=True, vmem_limit_bytes=48 << 20
        ),
        name="attention",
    )(
        queries,
        kv_cache.reshape(pages, kv_cache.shape[2], kv_cache.shape[3]),
        page_table.reshape(1, entries),
        jnp.repeat(lengths.astype(F32), page_table.shape[1]).reshape(1, entries),
        prefill_attn,
        out_weight,
        residual_in,
        norm_gain_in.reshape(1, -1),
        norm_gain_out.reshape(1, -1),
        expert_ids,
        route_weight,
        slot_table,
        w_gate_up,
        w_down,
    )
    return pl.pallas_call(
        functools.partial(expert_kernel, nz, nkv),
        out_shape=jax.ShapeDtypeStruct(residual_in.shape, BF16),
        in_specs=[vmem] * 3 + [hbm] * 2,
        out_specs=vmem,
        scratch_shapes=[
            pltpu.VMEM((nx, 2, 192, ff2), BF16),
            pltpu.VMEM((2, nx, ff, 256), BF16),
            pltpu.VMEM((ny, nz, 8, width + 128), BF16),
            pltpu.VMEM((ny, nz, 8, width), BF16),
            pltpu.VMEM((ny, nz, 8, width), BF16),
            pltpu.VMEM((nz, 8, width), BF16),
            pltpu.VMEM((nz, 8, width), BF16),
            pltpu.VMEM((8, width), BF16),
            pltpu.VMEM((nkv, 8, 256), BF16),
            dma(2),
            dma(2),
            dma(2),
            dma(nz),
            dma(nz),
            dma(ny),
            dma(ny),
            dma(ny),
            dma(ny),
            dma(nz),
            dma(nz),
            dma(nkv),
            dma(nkv),
        ],
        compiler_params=pltpu.CompilerParams(
            collective_id=1, has_side_effects=True, vmem_limit_bytes=48 << 20
        ),
        name="experts",
    )(block, middle, gain_out, wgu_all, wd_all)


def solution(mesh):
    in_specs = (
        P("pg", "kv"),
        P("pg", "kv"),
        P("pg", "kv"),
        P("pg", "kv", None, None),
        P(),
        P(),
        P("kv", None),
        P("kv"),
        P("kv"),
        P("pg", None),
        P("pg", None),
        P(),
        P("pg", "kv", None),
        P("pg", None, "kv"),
    )
    body = functools.partial(local, mesh.shape["pg"], mesh.shape["kv"])
    return jax.shard_map(
        body, mesh=mesh, in_specs=in_specs, out_specs=P("pg", "kv"), check_vma=False
    )
```

time: 590 us -> 156 us (0.26)
  blocking collectives: 330 us -> 0 us
  Pallas kernels: 0 us -> 141 us
  waiting for transfers between devices: 132 us -> 0 us
  other arithmetic: 67.9 us -> 0.68 us
  between operations: 13.5 us -> 0.06 us
  local copies, waits for them, and re-layouts: 23.6 us -> 11.8 us
  starting transfers between devices: 10.3 us -> 0 us
  matrix products: 8.78 us -> 0 us
    all_gather x3 -> x0, blocking collectives: 230 us -> none  [the longest x2 149 us: merged_2(): lax.all_gather(a.astype(kind), axis)]
    pallas_call x0 -> x2, Pallas kernels: none -> 141 us  [the longest x1 89.6 us: local(): pl.pallas_call(functools.partial(expert_kernel, nz, nkv), out_shape=jax.S...]
    unnamed x5 -> x0, waiting for transfers between devices: 81.1 us -> none
    all_to_all x3 -> x0, blocking collectives: 71 us -> none  [the longest x1 44.3 us: local(): lax.all_to_all(outgoing, 'pg', split_axis=0, concat_axis=0, tiled=True)]
    add x130 -> x0, other arithmetic: 63.6 us -> none  [the longest x63 61.7 us: merge_pair(): acc_a + acc_b]
    psum x2 -> x0, blocking collectives: 29.2 us -> none  [the longest x1 15.2 us: local(): out_squares = lax.psum(jnp.sum(mixed * mixed, axis=1), 'kv')]
    all_to_all x1 -> x0, waiting for transfers between devices: 29 us -> none  [local(): lax.all_to_all(narrowed, 'pg', split_axis=0, concat_axis=0, tiled=True)]
    all_gather x3 -> x0, waiting for transfers between devices: 21.6 us -> none  [the longest x1 21.6 us: merged_2(): lax.all_gather(a.astype(kind), axis)]
  transfers between devices with their start and end apart: 5 -> 0, of which waited for: 3 -> 0; matrix products, arithmetic and copies ran while one was open for 2% -> 0% of each run, Pallas kernels for 0% -> 0%
where the time goes in v1:
time: 156 us; the launch traced here: 153 us
  Pallas kernels  141 us (90%)
  local copies, waits for them, and re-layouts  11.8 us (8%)
    pallas_call x1, Pallas kernels, local(): pl.pallas_call(functools.partial(expert_kernel, nz, nkv), out_shape=jax.S...  89.6 us
    pallas_call x1, Pallas kernels, local(): pl.pallas_call(functools.partial(attention_kernel, nz, nkv), out_shape=(j...  51.3 us
    unnamed x22, local copies, waits for them, and re-layouts  11.4 us

profile of v1, /device:TPU:1, one launch (start us, length us, event | category | flops | bytes accessed | tf_op | source)
XLA Modules:
  0.0 153.4 jit_solution(4564587399927428167)
XLA Ops:
  0.0 0.7 convert_element_type.3
  0.7 0.8 copy.23.st_ref
  1.4 0.8 copy.21.ids_ref
  2.2 0.8 copy.22.rw_ref
  3.0 0.1 broadcast_in_dim.3
  3.1 0.1 reshape_reshape.3.le_ref
  3.2 0.8 copy.20
  4.0 0.1 reshape.13.pt_ref
  4.2 1.1 copy.24.wd_ref
  5.2 0.0 copy-start
  5.2 1.1 copy-done
  6.3 0.0 copy-start.1
  6.3 1.0 copy-done.1
  7.3 0.0 copy-start.2
  7.3 1.0 copy-done.2
  8.3 0.0 copy-start.3
  8.3 0.8 copy-done.3
  9.1 0.0 copy-start.4
  9.1 0.8 copy-done.4
  9.9 0.0 copy-start.5
  9.9 0.7 copy-done.5
  10.5 0.0 copy-start.6
  10.5 0.7 copy-done.6
  11.2 0.0 copy-start.7
  11.2 0.7 copy-done.7
  11.9 51.3 %attention.1 = (bf16[8,1664]{1,0:T(8,128)(2,1)S(1)}, f32[8,1536]{1,0:T(8,128)S(1)}, f32[1,1536]{1,0:T(1,128)S(1)}, bf16[4,192,1024]{2,1,0:T(8,128)(2,1)S(1)}, bf16[4,512,256]{2,1,0:T(8,128)(2,1)S(1)}) custom-call(bf16[4,192]{1,0:T(4,128)(2,1)S(1)} %copy-done.5, bf16[16,128,128]{2,1,0:T(8,128)(2,1)S(1)} %bitcast.3, s32[1,1024]{1,0:T(1,128)S(1)} %reshape.13.pt_ref, ...), custom_call_target="tpu_custom_call" | custom-call | tf_op jit(solution)/shard_map/attention/pallas_call | solution.py:709
  63.2 89.6 %experts.1 = bf16[64,192]{1,0:T(8,128)(2,1)S(1)} custom-call(bf16[8,1664]{1,0:T(8,128)(2,1)S(1)} %get-tuple-element.10.blk_ref, f32[8,1536]{1,0:T(8,128)S(1)} %get-tuple-element.11.mid_ref, f32[1,1536]{1,0:T(1,128)S(1)} %get-tuple-element.12.gout_ref, bf16[4,192,1024]{2,1,0:T(8,128)(2,1)S(1)} %get-tuple-element.13.wgu_all, ...), custom_call_target="tpu_custom_call" | custom-call | tf_op jit(solution)/shard_map/experts/pallas_call | solution.py:775
  152.8 0.6 copy.26
Async XLA Ops:
  5.2 1.1 copy-start
  6.3 1.0 copy-start.1
  7.3 1.0 copy-start.2
  8.3 0.8 copy-start.3
  9.1 0.8 copy-start.4
  9.9 0.7 copy-start.5
  10.5 0.7 copy-start.6
  11.2 0.7 copy-start.7

commit v2 on v0

v2 whole, which is shorter than its diff:
```python
import functools
import types
import jax
import jax.numpy as jnp
from jax import lax
from jax.experimental import pallas as pl
from jax.experimental.pallas import tpu as pltpu
from jax.sharding import PartitionSpec as P

NEG_FILL = -1e30
EPSILON = 1e-06
OFFSET = 4096.0
MESH = pl.DeviceIdType.MESH
NY = 4
F32 = jnp.float32
BF16 = jnp.bfloat16


def iota(shape, dim):
    return lax.broadcasted_iota(jnp.int32, shape, dim)


def remote(src, dst, ssem, rsem, dev):
    return pltpu.make_async_remote_copy(
        src_ref=src,
        dst_ref=dst,
        send_sem=ssem,
        recv_sem=rsem,
        device_id=dev,
        device_id_type=MESH,
    )


def greet(ny, nz, nkv, yy, zz, kk):
    barrier = pltpu.get_barrier_semaphore()

    def z_body(d, c):
        peer = yy * nz + lax.rem(zz + d, nz)
        pl.semaphore_signal(barrier, inc=1, device_id={"pg": peer}, device_id_type=MESH)
        return c

    lax.fori_loop(1, nz, z_body, 0)
    for d in range(1, ny):
        peer = lax.rem(yy + d, ny) * nz + zz
        pl.semaphore_signal(barrier, inc=1, device_id={"pg": peer}, device_id_type=MESH)
    for d in range(1, nkv):
        peer = lax.rem(kk + d, nkv)
        pl.semaphore_signal(barrier, inc=1, device_id={"kv": peer}, device_id_type=MESH)
    pl.semaphore_wait(barrier, nz - 1 + ny - 1 + nkv - 1)


def to_tiles(data):
    out = []
    for j in range(len(data) // 2):
        even, odd = data[2 * j], data[2 * j + 1]
        out.append(even[:, :128])
        out.append(even[:, 128:] + odd[:, :128])
        out.append(odd[:, 128:])
    return jnp.concatenate(out, axis=1)


def placement(parity, transposed=False):
    shape = (256, 192) if transposed else (192, 256)
    narrow, wide = (1, 0) if transposed else (0, 1)
    return (iota(shape, wide) == iota(shape, narrow) + 64 * parity).astype(BF16)


def stat_tile(x2):
    n = x2.shape[0]
    lane = iota((128, 256), 0) - 64
    head = iota((128, 256), 1) // 64
    pick = ((lane >= 0) & (lane < 9) & (lane % 3 == head) & (head < 3)).astype(BF16)
    spread = jnp.dot(x2, pick, preferred_element_type=F32)
    low = pltpu.roll(spread[:, :128], n - 4, 0)
    return jnp.where(iota((n, 128), 0) % 8 < 4, low, spread[:, 128:])


def split3(x):
    hi = x.astype(BF16).astype(F32)
    mid = (x - hi).astype(BF16).astype(F32)
    return hi, mid, x - hi - mid


def encode(acc, lse):
    n = acc.shape[0]
    sub, lane = iota((n, 128), 0) % 8, iota((n, 128), 1)
    down = pltpu.roll(lse, 4, 0)
    first = pltpu.roll(down, 64, 1)
    third = pltpu.roll(lse, 64, 1)
    which = (lane - 64) % 3
    value = jnp.where(which == 0, first, jnp.where(which == 1, down, third))
    hi, mid, lo = split3(value)
    part = (lane - 64) // 3
    stat = jnp.where(part == 0, hi, jnp.where(part == 1, mid, lo))
    is_stat = (sub >= 4) & (lane >= 64)
    return jnp.where(is_stat, jnp.where(lane < 73, stat, 0.0), acc).astype(BF16)


def merge(x):
    n, m, _ = x.shape
    flat = x.reshape(n * m, 128)
    lse = stat_tile(flat).reshape(n, m, 128)
    acc = flat.astype(F32).reshape(n, m, 128)
    top = jnp.max(lse, axis=0)
    weight = jnp.exp(lse - top[None])
    total = jnp.sum(weight, axis=0)
    return jnp.sum(weight * acc, axis=0) / total, top + jnp.log(total)


def layer_kernel(nz, nkv, names, *refs):
    s = types.SimpleNamespace(**dict(zip(names, refs)))
    ny, nx = NY, nkv // 2
    npg = ny * nz
    pg, kk = lax.axis_index("pg"), lax.axis_index("kv")
    yy, zz = pg // nz, lax.rem(pg, nz)
    xx, cc = kk // 2, lax.rem(kk, 2)
    sibling = kk + 1 - 2 * cc
    pages = s.kv.shape[0]
    rows = pages * 8
    width = s.w.shape[1]
    tops = s.ids.shape[0]
    own_req = s.q.shape[0]

    def z_peer(d):
        return lax.rem(zz + d, nz)

    def y_peer(d):
        return lax.rem(yy + d, ny)

    def k_peer(d):
        return lax.rem(kk + d, nkv)

    def at(y, z):
        return {"pg": y * nz + z}

    def loop(lo, hi, body):
        def step(i, c):
            body(i)
            return c

        lax.fori_loop(lo, hi, step, 0)

    loads = {}
    for n, name in enumerate(LOADED):
        loads[name] = pltpu.make_async_copy(
            getattr(s, name + "_in"), getattr(s, name), s.l_in.at[n]
        )
        loads[name].start()
    half = s.wgu.shape[1] // 2
    own_wg = pltpu.make_async_copy(s.wgu_in.at[0], s.wgu.at[kk], s.l_w.at[0])
    own_wd = pltpu.make_async_copy(s.wd_in.at[0], s.wd.at[kk], s.l_w.at[1])
    own_wg.start()
    own_wd.start()

    greet(ny, nz, nkv, yy, zz, kk)

    loads["q"].wait()
    q32 = s.q[...].astype(F32)
    s.qtile[...] = jnp.zeros_like(s.qtile)
    s.qtile[0:own_req, :] = q32[:, :128]
    s.qtile[4 : 4 + own_req, 0:64] = q32[:, 128:]
    s.qall[yy, zz] = s.qtile[...].astype(BF16)

    def q_copy(src_z, dst_z):
        ref = s.qall.at[yy, src_z]
        return remote(ref, ref, s.s_q.at[dst_z], s.r_q.at[src_z], at(yy, dst_z))

    loop(1, nz, lambda d: q_copy(zz, z_peer(nz - d)).start())

    def w_copies(src_g, src_d, k, n, dst_k):
        return (
            remote(src_g, s.wgu.at[k], s.s_wg.at[n], s.r_wg.at[k], {"kv": dst_k}),
            remote(src_d, s.wd.at[k], s.s_wd.at[n], s.r_wd.at[k], {"kv": dst_k}),
        )

    def block_of(d, core):
        return 2 * lax.rem(xx + d, nx) + core

    def own_copies():
        out = []
        for n, dst in enumerate((block_of(1, cc), block_of(3, cc), sibling)):
            out += w_copies(s.wgu_in.at[0], s.wd_in.at[0], kk, n, dst)
        return out

    def half_copies(d, n):
        k = block_of(d, cc)
        part = pl.ds(0 if d == 3 else half, half)
        dst = {"kv": block_of(1 if d == 3 else 3, cc)}
        h = 0 if d == 3 else 1
        return (
            remote(s.wgu.at[k, part], s.wgu.at[k, part], s.s_wg.at[n], s.r_fg.at[h], dst),
            remote(s.wd.at[k, part], s.wd.at[k, part], s.s_wd.at[n], s.r_fd.at[h], dst),
        )

    def far_arrivals():
        k = block_of(2, cc)
        out = []
        for h in range(2):
            part = pl.ds(h * half, half)
            out.append(
                remote(s.wgu.at[k, part], s.wgu.at[k, part], s.s_wg.at[7], s.r_fg.at[h], {"kv": k})
            )
            out.append(
                remote(s.wd.at[k, part], s.wd.at[k, part], s.s_wd.at[7], s.r_fd.at[h], {"kv": k})
            )
        return out

    def share_copies(d, n):
        k = block_of(d, cc)
        return w_copies(s.wgu.at[k], s.wd.at[k], k, n, sibling)

    def arrival(k):
        return w_copies(s.wgu.at[k], s.wd.at[k], k, 7, sibling)

    for copy in own_copies():
        copy.start()

    def weights_middle():
        for d, n in ((3, 3), (1, 4)):
            for copy in arrival(block_of(d, cc)):
                copy.wait_recv()
            for copy in half_copies(d, n):
                copy.start()
        for d, n in ((3, 5), (1, 6)):
            for copy in share_copies(d, n):
                copy.start()

    def weights_last():
        for copy in far_arrivals():
            copy.wait_recv()
        for copy in share_copies(2, 7):
            copy.start()
        own_wg.wait()
        own_wd.wait()
        for d in range(nx):
            for copy in arrival(block_of(d, 1 - cc)):
                copy.wait_recv()

    for name in ("res", "gi", "go", "pre", "w"):
        loads[name].wait()
    spread = placement(cc)
    s.ressend[...] = (
        jnp.dot(s.res[...], spread, preferred_element_type=F32)
        .astype(BF16)
        .reshape(s.ressend.shape)
    )
    s.gsend[...] = jnp.zeros_like(s.gsend)
    s.gsend[0:1, 0:192] = s.gi[...]
    s.gsend[1:2, 0:192] = s.go[...]
    gains = s.gsend[...]
    s.gsend[...] = jnp.where(cc == 1, pltpu.roll(gains, 64, 1), gains)

    def res_copy(src_k, dst_k):
        return remote(
            s.ressend.at[dst_k],
            s.resbuf.at[src_k],
            s.s_res.at[dst_k],
            s.r_res.at[src_k],
            {"kv": dst_k},
        )

    def g_copy(src_k, dst_k):
        return remote(s.gsend, s.gbuf.at[src_k], s.s_g.at[dst_k], s.r_g.at[src_k], {"kv": dst_k})

    for d in range(1, nkv):
        res_copy(kk, k_peer(d)).start()
        g_copy(kk, k_peer(d)).start()
    s.resbuf[kk] = s.ressend[kk]
    s.gbuf[kk] = s.gsend[...]

    s.pre_s[0:own_req, :] = jnp.zeros((own_req, s.pre_s.shape[1]), F32)
    s.pre_s[own_req:, :] = s.pre[...].astype(F32)
    done = jnp.dot(s.pre_s[...].astype(BF16), s.w[...], preferred_element_type=F32)
    s.proj[...] = done.astype(BF16).reshape(s.proj.shape)
    s.head_rows[...] = done[0:8]

    def rs_copy(src_k, dst_k):
        return remote(
            s.proj.at[dst_k], s.rsbuf.at[src_k], s.s_rs.at[dst_k], s.r_rs.at[src_k], {"kv": dst_k}
        )

    for k in range(1, nkv):

        @pl.when(kk != k)
        def _():
            rs_copy(kk, k).start()

    for name in ("ids", "rw", "st"):
        loads[name].wait()
    lane8, sub8 = iota((8, 128), 1), iota((8, 128), 0)
    s.turn[...] = jnp.full((8, 128), -1.0, F32)
    s.turn[0:2, 0 : s.st.shape[1]] = s.st[...].astype(F32)
    table = s.turn[...].T
    slot_lane = iota((128, 128), 1).astype(F32)
    expert = iota((128, 128), 0).astype(F32) + 1.0
    holder = [
        jnp.sum(jnp.where(table[:, j : j + 1] == slot_lane, expert, 0.0), axis=0, keepdims=True)
        - 1.0
        for j in range(2)
    ]
    s.turn[...] = jnp.full((8, 128), -2.0, F32)
    s.turn[0:tops, 0:64] = s.ids[...].astype(F32)
    s.ids_t[...] = s.turn[...].T
    s.turn[...] = jnp.zeros((8, 128), F32)
    s.turn[0:tops, 0:64] = s.rw[...]
    s.rw_t[...] = s.turn[...].T
    ids = s.ids_t[pl.ds(pl.multiple_of(8 * kk, 8), 8), :]
    gate = s.rw_t[pl.ds(pl.multiple_of(8 * kk, 8), 8), :]
    odd = iota((8, 1), 0) % 2 == 1
    dense = jnp.zeros((8, 128), F32)
    for j in range(tops):
        flip = odd if j % 2 == 0 else jnp.logical_not(odd)
        hit = ids[:, j : j + 1] == jnp.where(flip, holder[1], holder[0])
        dense = dense + jnp.where(hit, gate[:, j : j + 1], 0.0)
    dense_hi = dense.astype(BF16).astype(F32)
    dense_lo = pltpu.roll(dense - dense_hi, 64, 1)
    s.route[...] = jnp.where(lane8 < 64, dense_hi, dense_lo).astype(BF16)

    def xz_copy(src_z, dst_z):
        ref = s.xbuf.at[yy, src_z]
        return remote(ref, ref, s.s_xz.at[dst_z], s.r_xz.at[src_z], at(yy, dst_z))

    def xy_copy(src_y, dst_y, z):
        ref = s.xbuf.at[src_y, z]
        return remote(ref, ref, s.s_xy.at[dst_y, z], s.r_xy.at[src_y, z], at(dst_y, zz))

    def nth_z(i):
        off, sign = (i + 1) // 2, lax.rem(i, 2)
        return lax.rem(zz + sign * off + (1 - sign) * (nz - off), nz)

    def norm_and_send(near_first):
        for d in range(1, nkv):
            res_copy(k_peer(d), kk).wait_recv()
            g_copy(k_peer(d), kk).wait_recv()
        s.rsbuf[kk] = s.proj[kk]
        for d in range(1, nkv):
            rs_copy(k_peer(d), kk).wait_recv()
        gain = to_tiles([s.gbuf[k] for k in range(nkv)])
        residual = to_tiles([s.resbuf[k].astype(F32) for k in range(nkv)])
        projected = s.rsbuf[0].astype(F32)
        for k in range(1, nkv):
            projected = projected + s.rsbuf[k].astype(F32)
        middle = residual + projected
        square = jnp.sum(middle * middle, axis=1, keepdims=True) / width
        s.middle[...] = middle
        s.gain_out[...] = gain[1:2]
        normed = middle * lax.rsqrt(square + EPSILON) * gain[0:1]
        s.xbuf[yy, zz] = jnp.concatenate([normed.astype(BF16), s.route[...]], axis=1)
        if near_first:
            loop(1, nz, lambda i: xz_copy(zz, nth_z(i)).start())
        else:
            loop(1, nz, lambda i: xz_copy(zz, nth_z(nz - i)).start())

    def forward(lo, hi):
        def body(i):
            z = nth_z(i)
            if lo > 0:
                xz_copy(z, zz).wait_recv()
            for d in (2, 1, 3):
                xy_copy(yy, y_peer(d), z).start()

        if lo == 0:
            for d in (2, 1, 3):
                xy_copy(yy, y_peer(d), zz).start()
            lo = 1
        if hi > lo:
            loop(lo, hi, body)

    cut = [1, max(1, nz // 2), nz]

    loads["pt"].wait()
    loads["len"].wait()
    page_row = iota((rows, 1), 0) // 8
    head = iota((rows, 1), 0) % 8
    wide = (rows, s.pt.shape[1])
    request_lane = iota(wide, 1).astype(F32)
    cached_lane = s.len[...].astype(F32)
    owner, limit = jnp.zeros(wide, F32), jnp.zeros(wide, F32)
    for j in range(s.pt.shape[0]):
        mine = s.pt[j : j + 1, :] == page_row + pg * pages
        owner = owner + jnp.where(mine, request_lane, 0.0)
        limit = limit + jnp.where(mine, cached_lane - 128.0 * j, 0.0)
    owner = jnp.sum(owner, axis=1, keepdims=True)
    limit = jnp.sum(limit, axis=1, keepdims=True)
    owner_pg = jnp.floor(owner * 0.25)
    wanted = 8.0 * owner_pg + (owner - 4.0 * owner_pg) + jnp.where(head == 2, 4.0, 0.0)
    select = (iota((rows, npg * 8), 1).astype(F32) == wanted) & (head < 3)
    s.select[...] = select.astype(BF16)

    @pl.when(kk > 0)
    def _():
        norm_and_send(True)

    loop(1, nz, lambda d: q_copy(z_peer(d), zz).wait_recv())

    def qy_copy(src_y, dst_y):
        ref = s.qall.at[src_y]
        return remote(ref, ref, s.s_qy.at[dst_y], s.r_qy.at[src_y], at(dst_y, zz))

    for d in (2, 1, 3):
        qy_copy(yy, y_peer(d)).start()

    @pl.when(kk > 0)
    def _():
        forward(0, cut[0])

    loads["kv"].wait()
    for d in range(1, ny):
        qy_copy(y_peer(d), yy).wait_recv()

    lane = iota((rows, 128), 1)
    queries = jnp.dot(s.select[...], s.qall[...].reshape(npg * 8, 128), preferred_element_type=F32)
    queries = jnp.where(head == 1, pltpu.roll(queries, 64, 1), queries)
    queries = jnp.where(lane < 64, queries, 0.0)
    scores = jnp.concatenate(
        [
            lax.dot_general(
                queries[8 * i : 8 * i + 8].astype(BF16),
                s.kv[i],
                (((1,), (1,)), ((), ())),
                preferred_element_type=F32,
            )
            for i in range(pages)
        ],
        axis=0,
    ) * (64**-0.5)
    live = lane.astype(F32) < limit
    masked = jnp.where(live, scores, NEG_FILL)
    top = jnp.max(masked, axis=1, keepdims=True)
    probs = jnp.where(live, jnp.exp(masked - top), 0.0).astype(BF16).astype(F32)
    total = jnp.sum(probs, axis=1, keepdims=True)
    acc = jnp.concatenate(
        [
            jnp.dot(probs[8 * i : 8 * i + 8].astype(BF16), s.kv[i], preferred_element_type=F32)
            for i in range(pages)
        ],
        axis=0,
    )
    alive = limit > 0.0
    lse = jnp.where(alive, top + jnp.log(jnp.maximum(total, 1e-30)), NEG_FILL)
    acc = acc / jnp.where(alive, total, 1.0)

    eye = iota((rows, rows), 0) == iota((rows, rows), 1)
    owner_row = jnp.sum(jnp.where(eye, owner, 0.0), axis=0, keepdims=True)
    lse_row = jnp.sum(jnp.where(eye, lse, 0.0), axis=0, keepdims=True)
    head_row = iota((1, rows), 1) % 8
    group = (owner == owner_row) & (head == head_row) & (lse_row > -1e29)
    peak = jnp.max(jnp.where(group, lse_row, NEG_FILL), axis=1, keepdims=True)
    mass = jnp.sum(jnp.where(group, jnp.exp(lse_row - peak), 0.0), axis=1, keepdims=True)
    joint = peak + jnp.log(jnp.maximum(mass, 1e-30))
    acc = acc * jnp.where(alive, jnp.exp(lse - joint), 0.0)
    earlier = jnp.sum(
        jnp.where(group & (iota((rows, rows), 1) < iota((rows, rows), 0)), 1.0, 0.0),
        axis=1,
        keepdims=True,
    )
    code = jnp.where(alive & (earlier == 0.0), joint + OFFSET, 0.0)
    hi, mid, lo = split3(code)
    stats = jnp.where(
        lane == 64 + head,
        hi,
        jnp.where(lane == 67 + head, mid, jnp.where(lane == 70 + head, lo, 0.0)),
    )
    stats = jnp.where(head < 3, stats, 0.0)
    stats = pltpu.roll(stats, 3, 0) + pltpu.roll(stats, 2, 0) + pltpu.roll(stats, 1, 0)
    turned = pltpu.roll(acc, 64, 1)
    placed = jnp.where(
        head == 1,
        jnp.where(lane >= 64, acc, 0.0),
        jnp.where(lane < 64, turned, 0.0),
    )
    placed = jnp.where(head == 3, stats, placed)
    placed_hi = placed.astype(BF16)
    placed_lo = (placed - placed_hi.astype(F32)).astype(BF16)
    out_row = iota((npg * 8, rows), 0)
    request = ((out_row // 8) * 4 + out_row % 4).astype(F32)
    side = (out_row // 4) % 2
    head_all = iota((npg * 8, rows), 1) % 8
    scatter = (request == owner_row) & (head_all // 2 == side)
    scattered = jnp.dot(
        scatter.astype(BF16),
        jnp.concatenate([placed_hi, placed_lo], axis=1),
        preferred_element_type=F32,
    )
    s.part[...] = (scattered[:, :128] + scattered[:, 128:]).astype(BF16).reshape(s.part.shape)

    def py_copy(src_y, dst_y):
        return remote(
            s.part.at[dst_y], s.ybuf.at[src_y], s.s_py.at[dst_y], s.r_py.at[src_y], at(dst_y, zz)
        )

    for d in (2, 1, 3):
        py_copy(yy, y_peer(d)).start()
    s.ybuf[yy] = s.part[yy]
    weights_middle()
    for d in range(1, ny):
        py_copy(y_peer(d), yy).wait_recv()
    acc_y, lse_y = merge(s.ybuf[...].reshape(ny, nz * 8, 128))
    s.zsend[...] = encode(acc_y, lse_y).reshape(s.zsend.shape)

    def pz_copy(src_z, dst_z):
        return remote(
            s.zsend.at[dst_z], s.zbuf.at[src_z], s.s_pz.at[dst_z], s.r_pz.at[src_z], at(yy, dst_z)
        )

    loop(1, nz, lambda i: pz_copy(zz, nth_z(nz - i)).start())
    s.zbuf[zz] = s.zsend[zz]

    @pl.when(kk > 0)
    def _():
        forward(cut[0], cut[1])

    loop(1, nz, lambda d: pz_copy(z_peer(d), zz).wait_recv())
    attn, _ = merge(s.zbuf[...])
    attn = attn.astype(BF16).astype(F32)
    pair = jnp.where(sub8 < 4, attn, 0.0).astype(BF16)
    last = jnp.where((sub8 < 4) & (lane8 < 64), pltpu.roll(attn, 4, 0), 0.0).astype(BF16)
    dec = jnp.dot(pair, s.w[0:128, :], preferred_element_type=F32)
    dec = dec + jnp.dot(last[:, :64], s.w[128:192, :], preferred_element_type=F32)
    s.proj[0] = (s.head_rows[...] + dec).astype(BF16)

    @pl.when(kk != 0)
    def _():
        rs_copy(kk, 0).start()
        forward(cut[1], cut[2])

    @pl.when(kk == 0)
    def _():
        norm_and_send(False)
        forward(0, nz)

    weights_last()

    groups = min(4, nz)
    size = nz // groups
    order = sorted(range(groups), key=lambda g: -min(g, groups - g))

    def nth_group(g):
        return lax.rem(zz // size + g, groups)

    def oy_copy(src_y, dst_y, g):
        part = pl.ds(g * size, size)
        return remote(
            s.obuf.at[dst_y, part],
            s.oybuf.at[src_y, part],
            s.s_oy.at[dst_y, g],
            s.r_oy.at[src_y, g],
            at(dst_y, zz),
        )

    def experts(y):
        x = s.xbuf[y].reshape(nz * 8, width + 128)
        gate_up = jnp.dot(
            x[:, :width], s.wgu[...].reshape(width, s.wgu.shape[2]), preferred_element_type=F32
        )
        ff = gate_up.shape[1] // 2
        v = gate_up[:, :ff]
        hidden = (v / (1.0 + jnp.exp(-v)) * gate_up[:, ff:]).astype(BF16)
        produced = lax.dot_general(
            hidden,
            s.wd[...].reshape(width, ff),
            (((1,), (1,)), ((), ())),
            preferred_element_type=F32,
        )
        produced = produced.astype(BF16).astype(F32)
        share = jnp.where(iota((nz * 8, 128), 1) % 64 == pg, x[:, width:].astype(F32), 0.0)
        share = jnp.sum(share, axis=1, keepdims=True)
        s.obuf[y] = (produced * share).astype(BF16).reshape(nz, 8, width)

    for d in (0, 1, 3, 2):
        y = y_peer(d)
        if d > 0:
            loop(0, nz, lambda z: xy_copy(y, yy, z).wait_recv())
        experts(y)
        if d > 0:
            for g in order:
                oy_copy(yy, y, nth_group(g)).start()

    def oz_copy(src_z, dst_z):
        return remote(
            s.ozsend.at[dst_z], s.ozbuf.at[src_z], s.s_oz.at[dst_z], s.r_oz.at[src_z], at(yy, dst_z)
        )

    for g in order:
        first = nth_group(g) * size
        for d in range(1, ny):
            oy_copy(y_peer(d), yy, nth_group(g)).wait_recv()

        def add_y(i):
            z = first + i
            summed = s.obuf[yy, z].astype(F32)
            for d in range(1, ny):
                summed = summed + s.oybuf[y_peer(d), z].astype(F32)
            s.ozsend[z] = summed.astype(BF16)

            @pl.when(z != zz)
            def _():
                oz_copy(zz, z).start()

        loop(0, size, add_y)
    s.ozbuf[zz] = s.ozsend[zz]
    loop(1, nz, lambda d: oz_copy(z_peer(d), zz).wait_recv())
    mixed = s.middle[...]
    for z in range(nz):
        mixed = mixed + s.ozbuf[z].astype(F32)
    square = jnp.sum(mixed * mixed, axis=1, keepdims=True) / width
    s.fsend[...] = (mixed * lax.rsqrt(square + EPSILON) * s.gain_out[...]).astype(BF16)

    def f_copy(src_k, dst_k):
        start = pl.multiple_of(128 * (3 * (dst_k // 2) + lax.rem(dst_k, 2)), 128)
        return remote(
            s.fsend.at[:, pl.ds(start, 256)],
            s.fbuf.at[src_k],
            s.s_f.at[dst_k],
            s.r_f.at[src_k],
            {"kv": dst_k},
        )

    for d in range(1, nkv):
        f_copy(kk, k_peer(d)).start()
    s.fbuf[kk] = s.fsend[:, pl.ds(pl.multiple_of(128 * (3 * xx + cc), 128), 256)]

    def z_sent(d):
        peer = z_peer(d)
        q_copy(zz, peer).wait_send()
        pz_copy(zz, peer).wait_send()
        xz_copy(zz, peer).wait_send()
        oz_copy(zz, peer).wait_send()

    loop(1, nz, z_sent)
    for d in range(1, ny):
        peer = y_peer(d)
        qy_copy(yy, peer).wait_send()
        py_copy(yy, peer).wait_send()
        loop(0, nz, lambda z: xy_copy(yy, peer, z).wait_send())
        loop(0, groups, lambda g: oy_copy(yy, peer, g).wait_send())
    for d in range(1, nkv):
        peer = k_peer(d)
        res_copy(kk, peer).wait_send()
        g_copy(kk, peer).wait_send()
        rs_copy(kk, peer).wait_send()
    for copy in own_copies():
        copy.wait_send()
    for copy in half_copies(3, 3) + half_copies(1, 4):
        copy.wait_send()
    for copy in share_copies(3, 5) + share_copies(1, 6) + share_copies(2, 7):
        copy.wait_send()

    for d in range(1, nkv):
        f_copy(k_peer(d), kk).wait_recv()
    s.out_v[...] = jnp.dot(
        s.fbuf[...].reshape(nkv * 8, 256), placement(cc, True), preferred_element_type=F32
    ).astype(BF16)
    for d in range(1, nkv):
        f_copy(kk, k_peer(d)).wait_send()


INPUTS = ("res", "q", "pre", "kv", "pt", "len", "w", "gi", "go", "ids", "rw", "st", "wgu", "wd")
LOADED = ("q", "res", "gi", "go", "pre", "w", "ids", "rw", "st", "pt", "len", "kv")


def dma(*shape):
    return pltpu.SemaphoreType.DMA(shape)


def local(
    npg,
    nkv,
    residual_in,
    queries,
    prefill_attn,
    kv_cache,
    page_table,
    lengths,
    out_weight,
    norm_gain_in,
    norm_gain_out,
    expert_ids,
    route_weight,
    slot_table,
    w_gate_up,
    w_down,
):
    ny, nz = NY, npg // NY
    width = out_weight.shape[1]
    ff2, ff = w_gate_up.shape[2], w_down.shape[1]
    groups = min(4, nz)
    args = (
        residual_in,
        queries,
        prefill_attn,
        kv_cache.reshape(kv_cache.shape[0], kv_cache.shape[2], kv_cache.shape[3]),
        page_table.T,
        lengths.reshape(1, -1),
        out_weight,
        norm_gain_in.reshape(1, -1),
        norm_gain_out.reshape(1, -1),
        expert_ids.T,
        route_weight.T,
        slot_table.T,
        w_gate_up,
        w_down.swapaxes(1, 2),
    )
    by_name = dict(zip(INPUTS, args))
    V = pltpu.VMEM
    scratch = {name: V(by_name[name].shape, by_name[name].dtype) for name in LOADED}
    scratch.update(
        wgu=V((nkv, 192, ff2), BF16),
        wd=V((nkv, 192, ff), BF16),
        qtile=V((8, 128), F32),
        qall=V((ny, nz, 8, 128), BF16),
        select=V((by_name["kv"].shape[0] * 8, npg * 8), BF16),
        part=V((ny, nz, 8, 128), BF16),
        ybuf=V((ny, nz, 8, 128), BF16),
        zsend=V((nz, 8, 128), BF16),
        zbuf=V((nz, 8, 128), BF16),
        pre_s=V((64, 192), F32),
        head_rows=V((8, width), F32),
        proj=V((nkv, 8, width), BF16),
        rsbuf=V((nkv, 8, width), BF16),
        ressend=V((nkv, 8, 256), BF16),
        resbuf=V((nkv, 8, 256), BF16),
        gsend=V((8, 256), F32),
        gbuf=V((nkv, 8, 256), F32),
        turn=V((8, 128), F32),
        ids_t=V((128, 8), F32),
        rw_t=V((128, 8), F32),
        route=V((8, 128), BF16),
        middle=V((8, width), F32),
        gain_out=V((1, width), F32),
        xbuf=V((ny, nz, 8, width + 128), BF16),
        obuf=V((ny, nz, 8, width), BF16),
        oybuf=V((ny, nz, 8, width), BF16),
        ozsend=V((nz, 8, width), BF16),
        ozbuf=V((nz, 8, width), BF16),
        fsend=V((8, width), BF16),
        fbuf=V((nkv, 8, 256), BF16),
        l_in=dma(len(LOADED)),
        l_w=dma(2),
        s_wg=dma(8),
        s_wd=dma(8),
        r_wg=dma(nkv),
        r_wd=dma(nkv),
        r_fg=dma(2),
        r_fd=dma(2),
        s_xy=dma(ny, nz),
        r_xy=dma(ny, nz),
        s_oy=dma(ny, groups),
        r_oy=dma(ny, groups),
    )
    for name, n in (
        ("q", nz),
        ("pz", nz),
        ("xz", nz),
        ("oz", nz),
        ("qy", ny),
        ("py", ny),
        ("rs", nkv),
        ("res", nkv),
        ("g", nkv),
        ("f", nkv),
    ):
        scratch["s_" + name] = dma(n)
        scratch["r_" + name] = dma(n)
    names = [name + "_in" for name in INPUTS] + ["out_v"] + list(scratch)
    return pl.pallas_call(
        functools.partial(layer_kernel, nz, nkv, names),
        out_shape=jax.ShapeDtypeStruct(residual_in.shape, BF16),
        in_specs=[pl.BlockSpec(memory_space=pltpu.HBM)] * len(args),
        out_specs=pl.BlockSpec(memory_space=pltpu.VMEM),
        scratch_shapes=list(scratch.values()),
        compiler_params=pltpu.CompilerParams(
            collective_id=0, has_side_effects=True, vmem_limit_bytes=56 << 20
        ),
        name="layer",
    )(*args)


def solution(mesh):
    in_specs = (
        P("pg", "kv"),
        P("pg", "kv"),
        P("pg", "kv"),
        P("pg", "kv", None, None),
        P(),
        P(),
        P("kv", None),
        P("kv"),
        P("kv"),
        P("pg", None),
        P("pg", None),
        P(),
        P("pg", "kv", None),
        P("pg", None, "kv"),
    )
    body = functools.partial(local, mesh.shape["pg"], mesh.shape["kv"])
    return jax.shard_map(
        body, mesh=mesh, in_specs=in_specs, out_specs=P("pg", "kv"), check_vma=False
    )
```

time: 590 us -> 120 us (0.20)
  blocking collectives: 330 us -> 0 us
  waiting for transfers between devices: 132 us -> 0 us
  Pallas kernels: 0 us -> 119 us
  other arithmetic: 67.9 us -> 0 us
  local copies, waits for them, and re-layouts: 23.6 us -> 1.38 us
  between operations: 13.5 us -> 0.01 us
  starting transfers between devices: 10.3 us -> 0 us
  matrix products: 8.78 us -> 0 us
    all_gather x3 -> x0, blocking collectives: 230 us -> none  [the longest x2 149 us: merged_2(): lax.all_gather(a.astype(kind), axis)]
    pallas_call x0 -> x1, Pallas kernels: none -> 119 us  [local(): pl.pallas_call(functools.partial(layer_kernel, nz, nkv, names), out_shape...]
    unnamed x5 -> x0, waiting for transfers between devices: 81.1 us -> none
    all_to_all x3 -> x0, blocking collectives: 71 us -> none  [the longest x1 44.3 us: local(): lax.all_to_all(outgoing, 'pg', split_axis=0, concat_axis=0, tiled=True)]
    add x130 -> x0, other arithmetic: 63.6 us -> none  [the longest x63 61.7 us: merge_pair(): acc_a + acc_b]
    psum x2 -> x0, blocking collectives: 29.2 us -> none  [the longest x1 15.2 us: local(): out_squares = lax.psum(jnp.sum(mixed * mixed, axis=1), 'kv')]
    all_to_all x1 -> x0, waiting for transfers between devices: 29 us -> none  [local(): lax.all_to_all(narrowed, 'pg', split_axis=0, concat_axis=0, tiled=True)]
    all_gather x3 -> x0, waiting for transfers between devices: 21.6 us -> none  [the longest x1 21.6 us: merged_2(): lax.all_gather(a.astype(kind), axis)]
  transfers between devices with their start and end apart: 5 -> 0, of which waited for: 3 -> 0; matrix products, arithmetic and copies ran while one was open for 2% -> 0% of each run, Pallas kernels for 0% -> 0%
where the time goes in v2:
time: 120 us
  Pallas kernels  119 us (99%)
  local copies, waits for them, and re-layouts  1.38 us (1%)
    pallas_call x1, Pallas kernels, local(): pl.pallas_call(functools.partial(layer_kernel, nz, nkv, names), out_shape...  119 us

profile of v2, /device:TPU:1, one launch (start us, length us, event | category | flops | bytes accessed | tf_op | source)
XLA Modules:
  0.0 120.0 jit_solution(12597407731934553744)
XLA Ops:
  0.0 118.6 %layer.1 = bf16[64,192]{1,0:T(8,128)(2,1)} custom-call(bf16[64,192]{1,0:T(8,128)(2,1)} %refs_0_.1, bf16[4,192]{1,0:T(4,128)(2,1)} %refs_1_.1, bf16[60,192]{1,0:T(8,128)(2,1)} %refs_2_.1, bf16[16,128,128]{2,1,0:T(8,128)(2,1)} %bitcast.9, s32[4,256]{1,0:T(4,128)} %bitcast.11, s32[1,256]{1,0:T(1,128)} %bitcast.14, bf16[192,1536]{1,0:T(8,128)(2,1)} %refs_6_.1, ...), custom_call_target="tpu_custom_call" | custom-call | tf_op jit(solution)/shard_map/layer/pallas_call | solution.py:766
  118.6 1.4 %copy.16 = bf16[64,192]{1,0:T(8,128)(2,1)} copy(bf16[64,192]{1,0:T(8,128)(2,1)} %layer.1) | data formatting | bytes 49152

commit v3 on v2

--- a/solution.py
+++ b/solution.py
@@ -46,7 +46,7 @@
     for d in range(1, nkv):
         peer = lax.rem(kk + d, nkv)
         pl.semaphore_signal(barrier, inc=1, device_id={"kv": peer}, device_id_type=MESH)
-    pl.semaphore_wait(barrier, nz - 1 + ny - 1 + nkv - 1)
+    return barrier, nz - 1 + ny - 1 + nkv - 1
 
 
 def to_tiles(data):
@@ -152,7 +152,7 @@
     own_wg.start()
     own_wd.start()
 
-    greet(ny, nz, nkv, yy, zz, kk)
+    barrier, callers = greet(ny, nz, nkv, yy, zz, kk)
 
     loads["q"].wait()
     q32 = s.q[...].astype(F32)
@@ -165,7 +165,6 @@
         ref = s.qall.at[yy, src_z]
         return remote(ref, ref, s.s_q.at[dst_z], s.r_q.at[src_z], at(yy, dst_z))
 
-    loop(1, nz, lambda d: q_copy(zz, z_peer(nz - d)).start())
 
     def w_copies(src_g, src_d, k, n, dst_k):
         return (
@@ -212,9 +211,6 @@
     def arrival(k):
         return w_copies(s.wgu.at[k], s.wd.at[k], k, 7, sibling)
 
-    for copy in own_copies():
-        copy.start()
-
     def weights_middle():
         for d, n in ((3, 3), (1, 4)):
             for copy in arrival(block_of(d, cc)):
@@ -262,9 +258,6 @@
     def g_copy(src_k, dst_k):
         return remote(s.gsend, s.gbuf.at[src_k], s.s_g.at[dst_k], s.r_g.at[src_k], {"kv": dst_k})
 
-    for d in range(1, nkv):
-        res_copy(kk, k_peer(d)).start()
-        g_copy(kk, k_peer(d)).start()
     s.resbuf[kk] = s.ressend[kk]
     s.gbuf[kk] = s.gsend[...]
 
@@ -272,18 +265,12 @@
     s.pre_s[own_req:, :] = s.pre[...].astype(F32)
     done = jnp.dot(s.pre_s[...].astype(BF16), s.w[...], preferred_element_type=F32)
     s.proj[...] = done.astype(BF16).reshape(s.proj.shape)
-    s.head_rows[...] = done[0:8]
 
     def rs_copy(src_k, dst_k):
         return remote(
             s.proj.at[dst_k], s.rsbuf.at[src_k], s.s_rs.at[dst_k], s.r_rs.at[src_k], {"kv": dst_k}
         )
 
-    for k in range(1, nkv):
-
-        @pl.when(kk != k)
-        def _():
-            rs_copy(kk, k).start()
 
     for name in ("ids", "rw", "st"):
         loads[name].wait()
@@ -316,57 +303,224 @@
     dense_lo = pltpu.roll(dense - dense_hi, 64, 1)
     s.route[...] = jnp.where(lane8 < 64, dense_hi, dense_lo).astype(BF16)
 
-    def xz_copy(src_z, dst_z):
-        ref = s.xbuf.at[yy, src_z]
-        return remote(ref, ref, s.s_xz.at[dst_z], s.r_xz.at[src_z], at(yy, dst_z))
-
-    def xy_copy(src_y, dst_y, z):
-        ref = s.xbuf.at[src_y, z]
-        return remote(ref, ref, s.s_xy.at[dst_y, z], s.r_xy.at[src_y, z], at(dst_y, zz))
+    fold = width // 2
+    groups = min(4, nz)
+    size = nz // groups
+    order = sorted(range(groups), key=lambda g: -min(g, groups - g))
+    two_stage = nz == 16
 
     def nth_z(i):
         off, sign = (i + 1) // 2, lax.rem(i, 2)
         return lax.rem(zz + sign * off + (1 - sign) * (nz - off), nz)
 
-    def norm_and_send(near_first):
+    def nth_group(g):
+        return lax.rem(zz // size + g, groups)
+
+    def make_pass(tag, folded):
+        p = types.SimpleNamespace(
+            **{name: getattr(s, name + "_" + tag) for name in PASS_SCRATCH}
+        )
+        relayed = two_stage and not folded
+        cols = fold if folded else width
+
+        def xz_copy(src_z, dst_z, sem=None):
+            ref = p.x.at[yy, src_z]
+            sem = p.s_xz.at[dst_z] if sem is None else p.s_xr.at[sem]
+            return remote(ref, ref, sem, p.r_xz.at[src_z], at(yy, dst_z))
+
+        def xy_copy(src_y, dst_y, z):
+            ref = p.x.at[src_y, z]
+            return remote(ref, ref, p.s_xy.at[dst_y, z], p.r_xy.at[src_y, z], at(dst_y, zz))
+
+        def oy_copy(src_y, dst_y, g):
+            part = pl.ds(g * size, size)
+            return remote(
+                p.o.at[dst_y, part],
+                p.oy.at[src_y, part],
+                p.s_oy.at[dst_y, g],
+                p.r_oy.at[src_y, g],
+                at(dst_y, zz),
+            )
+
+        def oz_copy(src_z, dst_z):
+            return remote(
+                p.os.at[dst_z], p.ob.at[src_z], p.s_oz.at[dst_z], p.r_oz.at[src_z], at(yy, dst_z)
+            )
+
+        def relays(i):
+            src = nth_z(i)
+            hops = (-1, -2, -3) if i == 7 else (1, 2, 3, 4)
+            first = 0 if i == 7 else 3
+            return [
+                xz_copy(src, lax.rem(zz + h + nz, nz), first + n) for n, h in enumerate(hops)
+            ]
+
+        near = 9 if relayed else nz
+
+        def send(rows):
+            p.x[yy, zz] = rows
+            loop(1, near, lambda i: xz_copy(zz, nth_z(near - i)).start())
+
+        def forward(lo, hi):
+            def one(i):
+                z = nth_z(i)
+                xz_copy(z, zz).wait_recv()
+                for d in (2, 1, 3):
+                    xy_copy(yy, y_peer(d), z).start()
+
+            if lo == 0:
+                for d in (2, 1, 3):
+                    xy_copy(yy, y_peer(d), zz).start()
+                lo = 1
+            if relayed and lo < 9 <= hi:
+                for i in (7, 8):
+                    xz_copy(nth_z(i), zz).wait_recv()
+                    for copy in relays(i):
+                        copy.start()
+                loop(lo, 7, one)
+                for i in (7, 8):
+                    for d in (2, 1, 3):
+                        xy_copy(yy, y_peer(d), nth_z(i)).start()
+                lo = 9
+            if hi > lo:
+                loop(lo, hi, one)
+
+        def mlp(x, share):
+            gate_up = jnp.dot(
+                x, s.wgu[...].reshape(width, s.wgu.shape[2]), preferred_element_type=F32
+            )
+            ff = gate_up.shape[1] // 2
+            v = gate_up[:, :ff]
+            hidden = (v / (1.0 + jnp.exp(-v)) * gate_up[:, ff:]).astype(BF16)
+            produced = lax.dot_general(
+                hidden,
+                s.wd[...].reshape(width, ff),
+                (((1,), (1,)), ((), ())),
+                preferred_element_type=F32,
+            )
+            mine = jnp.where(iota(share.shape, 1) % 64 == pg, share, 0.0)
+            return produced.astype(BF16).astype(F32) * jnp.sum(mine, axis=1, keepdims=True)
+
+        def experts_of(y):
+            x = p.x[y].reshape(nz * 8, cols + 128)
+            p.o[y] = mlp(x[:, :cols], x[:, cols:].astype(F32)).astype(BF16).reshape(nz, 8, cols)
+
+        def experts_of_pair(ya, yb):
+            n = nz * 8
+            xa = p.x[ya].reshape(n, cols + 128).astype(F32)
+            xb = p.x[yb].reshape(n, cols + 128).astype(F32)
+            first = iota((n, cols), 0) % 8 < 4
+            low = jnp.where(first, xa[:, :cols], pltpu.roll(xb[:, :cols], 4, 0))
+            high = jnp.where(first, pltpu.roll(xa[:, :cols], n - 4, 0), xb[:, :cols])
+            share = jnp.where(first[:, :128], xa[:, cols:], pltpu.roll(xb[:, cols:], 4, 0))
+            out = mlp(jnp.concatenate([low, high], axis=1).astype(BF16), share)
+            low, high = out[:, :cols], out[:, cols:]
+            oa = jnp.where(first, low, pltpu.roll(high, 4, 0))
+            ob = jnp.where(first, pltpu.roll(low, n - 4, 0), high)
+            p.o[ya] = oa.astype(BF16).reshape(nz, 8, cols)
+            p.o[yb] = ob.astype(BF16).reshape(nz, 8, cols)
+
+        def arrived(d):
+            if d > 0:
+                loop(0, nz, lambda z: xy_copy(y_peer(d), yy, z).wait_recv())
+
+        def go_back(d):
+            if d > 0:
+                for g in order:
+                    oy_copy(yy, y_peer(d), nth_group(g)).start()
+
+        def experts():
+            for pair in ((0, 1), (3, 2)):
+                if folded:
+                    arrived(pair[0])
+                    arrived(pair[1])
+                    experts_of_pair(y_peer(pair[0]), y_peer(pair[1]))
+                    go_back(pair[0])
+                    go_back(pair[1])
+                else:
+                    for d in pair:
+                        arrived(d)
+                        experts_of(y_peer(d))
+                        go_back(d)
+
+        def sums():
+            for g in order:
+                first = nth_group(g) * size
+                for d in range(1, ny):
+                    oy_copy(y_peer(d), yy, nth_group(g)).wait_recv()
+
+                def add_y(i):
+                    z = first + i
+                    summed = p.o[yy, z].astype(F32)
+                    for d in range(1, ny):
+                        summed = summed + p.oy[y_peer(d), z].astype(F32)
+                    p.os[z] = summed.astype(BF16)
+
+                    @pl.when(z != zz)
+                    def _():
+                        oz_copy(zz, z).start()
+
+                loop(0, size, add_y)
+            p.ob[zz] = p.os[zz]
+
+        def collect():
+            loop(1, nz, lambda d: oz_copy(z_peer(d), zz).wait_recv())
+            total = p.ob[0].astype(F32)
+            for z in range(1, nz):
+                total = total + p.ob[z].astype(F32)
+            return total
+
+        def finish():
+            loop(1, near, lambda i: xz_copy(zz, nth_z(i)).wait_send())
+            if relayed:
+                for i in (7, 8):
+                    for copy in relays(i):
+                        copy.wait_send()
+            for d in range(1, ny):
+                peer = y_peer(d)
+                loop(0, nz, lambda z: xy_copy(yy, peer, z).wait_send())
+                loop(0, groups, lambda g: oy_copy(yy, peer, g).wait_send())
+            loop(1, nz, lambda d: oz_copy(zz, z_peer(d)).wait_send())
+
+        return types.SimpleNamespace(
+            send=send,
+            forward=forward,
+            experts=experts,
+            sums=sums,
+            collect=collect,
+            finish=finish,
+        )
+
+    full, early, late = make_pass("a", False), make_pass("b", True), make_pass("c", True)
+    low4 = iota((8, fold), 0) < 4
+
+    def folded_rows(x, first):
+        low, high = x[:, :fold], x[:, fold:]
+        if first == 0:
+            return jnp.where(low4, low, pltpu.roll(high, 4, 0))
+        return jnp.where(low4, pltpu.roll(low, 4, 0), high)
+
+    def normed_rows(middle):
+        square = jnp.sum(middle * middle, axis=1, keepdims=True) / width
+        return middle * lax.rsqrt(square + EPSILON) * s.gains[0:1]
+
+    def early_rows():
         for d in range(1, nkv):
             res_copy(k_peer(d), kk).wait_recv()
             g_copy(k_peer(d), kk).wait_recv()
         s.rsbuf[kk] = s.proj[kk]
         for d in range(1, nkv):
             rs_copy(k_peer(d), kk).wait_recv()
-        gain = to_tiles([s.gbuf[k] for k in range(nkv)])
-        residual = to_tiles([s.resbuf[k].astype(F32) for k in range(nkv)])
+        s.gains[...] = to_tiles([s.gbuf[k] for k in range(nkv)])
+        middle = to_tiles([s.resbuf[k].astype(F32) for k in range(nkv)])
         projected = s.rsbuf[0].astype(F32)
         for k in range(1, nkv):
             projected = projected + s.rsbuf[k].astype(F32)
-        middle = residual + projected
-        square = jnp.sum(middle * middle, axis=1, keepdims=True) / width
+        middle = middle + projected
         s.middle[...] = middle
-        s.gain_out[...] = gain[1:2]
-        normed = middle * lax.rsqrt(square + EPSILON) * gain[0:1]
-        s.xbuf[yy, zz] = jnp.concatenate([normed.astype(BF16), s.route[...]], axis=1)
-        if near_first:
-            loop(1, nz, lambda i: xz_copy(zz, nth_z(i)).start())
-        else:
-            loop(1, nz, lambda i: xz_copy(zz, nth_z(nz - i)).start())
-
-    def forward(lo, hi):
-        def body(i):
-            z = nth_z(i)
-            if lo > 0:
-                xz_copy(z, zz).wait_recv()
-            for d in (2, 1, 3):
-                xy_copy(yy, y_peer(d), z).start()
-
-        if lo == 0:
-            for d in (2, 1, 3):
-                xy_copy(yy, y_peer(d), zz).start()
-            lo = 1
-        if hi > lo:
-            loop(lo, hi, body)
-
-    cut = [1, max(1, nz // 2), nz]
+        s.normed[...] = normed_rows(middle)
+
+    near_half = min(9, nz)
 
     loads["pt"].wait()
     loads["len"].wait()
@@ -387,9 +541,15 @@
     select = (iota((rows, npg * 8), 1).astype(F32) == wanted) & (head < 3)
     s.select[...] = select.astype(BF16)
 
-    @pl.when(kk > 0)
-    def _():
-        norm_and_send(True)
+    pl.semaphore_wait(barrier, callers)
+    loop(1, nz, lambda d: q_copy(zz, z_peer(nz - d)).start())
+    for d in range(1, nkv):
+        rs_copy(kk, k_peer(d)).start()
+    for d in range(1, nkv):
+        res_copy(kk, k_peer(d)).start()
+        g_copy(kk, k_peer(d)).start()
+    for copy in own_copies():
+        copy.start()
 
     loop(1, nz, lambda d: q_copy(z_peer(d), zz).wait_recv())
 
@@ -400,9 +560,18 @@
     for d in (2, 1, 3):
         qy_copy(yy, y_peer(d)).start()
 
+    early_rows()
+
     @pl.when(kk > 0)
     def _():
-        forward(0, cut[0])
+        full.send(jnp.concatenate([s.normed[...].astype(BF16), s.route[...]], axis=1))
+
+    @pl.when(kk == 0)
+    def _():
+        route = pltpu.roll(s.route[...].astype(F32), 4, 0).astype(BF16)
+        rows4 = folded_rows(s.normed[...], 4).astype(BF16)
+        early.send(jnp.concatenate([rows4, route], axis=1))
+
 
     loads["kv"].wait()
     for d in range(1, ny):
@@ -492,7 +661,15 @@
     for d in (2, 1, 3):
         py_copy(yy, y_peer(d)).start()
     s.ybuf[yy] = s.part[yy]
-    weights_middle()
+
+    @pl.when(kk > 0)
+    def _():
+        full.forward(0, near_half)
+
+    @pl.when(kk == 0)
+    def _():
+        early.forward(0, 1)
+
     for d in range(1, ny):
         py_copy(y_peer(d), yy).wait_recv()
     acc_y, lse_y = merge(s.ybuf[...].reshape(ny, nz * 8, 128))
@@ -505,10 +682,16 @@
 
     loop(1, nz, lambda i: pz_copy(zz, nth_z(nz - i)).start())
     s.zbuf[zz] = s.zsend[zz]
+    weights_middle()
 
     @pl.when(kk > 0)
     def _():
-        forward(cut[0], cut[1])
+        if nz > near_half:
+            full.forward(near_half, nz)
+
+    @pl.when(kk == 0)
+    def _():
+        early.forward(1, nz)
 
     loop(1, nz, lambda d: pz_copy(z_peer(d), zz).wait_recv())
     attn, _ = merge(s.zbuf[...])
@@ -517,94 +700,44 @@
     last = jnp.where((sub8 < 4) & (lane8 < 64), pltpu.roll(attn, 4, 0), 0.0).astype(BF16)
     dec = jnp.dot(pair, s.w[0:128, :], preferred_element_type=F32)
     dec = dec + jnp.dot(last[:, :64], s.w[128:192, :], preferred_element_type=F32)
-    s.proj[0] = (s.head_rows[...] + dec).astype(BF16)
+    s.decsend[...] = folded_rows(dec, 0).astype(BF16)
+
+    def dec_copy(src_k):
+        return remote(s.decsend, s.decbuf.at[src_k], s.s_dec.at[0], s.r_dec.at[src_k], {"kv": 0})
+
+    def finished(mixed):
+        square = jnp.sum(mixed * mixed, axis=1, keepdims=True) / width
+        s.fsend[...] = (mixed * lax.rsqrt(square + EPSILON) * s.gains[1:2]).astype(BF16)
 
     @pl.when(kk != 0)
     def _():
-        rs_copy(kk, 0).start()
-        forward(cut[1], cut[2])
+        dec_copy(kk).start()
+        weights_last()
+        full.experts()
+        full.sums()
+        finished(s.middle[...] + full.collect())
 
     @pl.when(kk == 0)
     def _():
-        norm_and_send(False)
-        forward(0, nz)
-
-    weights_last()
-
-    groups = min(4, nz)
-    size = nz // groups
-    order = sorted(range(groups), key=lambda g: -min(g, groups - g))
-
-    def nth_group(g):
-        return lax.rem(zz // size + g, groups)
-
-    def oy_copy(src_y, dst_y, g):
-        part = pl.ds(g * size, size)
-        return remote(
-            s.obuf.at[dst_y, part],
-            s.oybuf.at[src_y, part],
-            s.s_oy.at[dst_y, g],
-            s.r_oy.at[src_y, g],
-            at(dst_y, zz),
-        )
-
-    def experts(y):
-        x = s.xbuf[y].reshape(nz * 8, width + 128)
-        gate_up = jnp.dot(
-            x[:, :width], s.wgu[...].reshape(width, s.wgu.shape[2]), preferred_element_type=F32
-        )
-        ff = gate_up.shape[1] // 2
-        v = gate_up[:, :ff]
-        hidden = (v / (1.0 + jnp.exp(-v)) * gate_up[:, ff:]).astype(BF16)
-        produced = lax.dot_general(
-            hidden,
-            s.wd[...].reshape(width, ff),
-            (((1,), (1,)), ((), ())),
-            preferred_element_type=F32,
-        )
-        produced = produced.astype(BF16).astype(F32)
-        share = jnp.where(iota((nz * 8, 128), 1) % 64 == pg, x[:, width:].astype(F32), 0.0)
-        share = jnp.sum(share, axis=1, keepdims=True)
-        s.obuf[y] = (produced * share).astype(BF16).reshape(nz, 8, width)
-
-    for d in (0, 1, 3, 2):
-        y = y_peer(d)
-        if d > 0:
-            loop(0, nz, lambda z: xy_copy(y, yy, z).wait_recv())
-        experts(y)
-        if d > 0:
-            for g in order:
-                oy_copy(yy, y, nth_group(g)).start()
-
-    def oz_copy(src_z, dst_z):
-        return remote(
-            s.ozsend.at[dst_z], s.ozbuf.at[src_z], s.s_oz.at[dst_z], s.r_oz.at[src_z], at(yy, dst_z)
-        )
-
-    for g in order:
-        first = nth_group(g) * size
-        for d in range(1, ny):
-            oy_copy(y_peer(d), yy, nth_group(g)).wait_recv()
-
-        def add_y(i):
-            z = first + i
-            summed = s.obuf[yy, z].astype(F32)
-            for d in range(1, ny):
-                summed = summed + s.oybuf[y_peer(d), z].astype(F32)
-            s.ozsend[z] = summed.astype(BF16)
-
-            @pl.when(z != zz)
-            def _():
-                oz_copy(zz, z).start()
-
-        loop(0, size, add_y)
-    s.ozbuf[zz] = s.ozsend[zz]
-    loop(1, nz, lambda d: oz_copy(z_peer(d), zz).wait_recv())
-    mixed = s.middle[...]
-    for z in range(nz):
-        mixed = mixed + s.ozbuf[z].astype(F32)
-    square = jnp.sum(mixed * mixed, axis=1, keepdims=True) / width
-    s.fsend[...] = (mixed * lax.rsqrt(square + EPSILON) * s.gain_out[...]).astype(BF16)
+        decoded = s.decsend[...].astype(F32)
+        for k in range(1, nkv):
+            dec_copy(k).wait_recv()
+            decoded = decoded + s.decbuf[k].astype(F32)
+        spread4 = jnp.concatenate([decoded, pltpu.roll(decoded, 4, 0)], axis=1)
+        middle = s.middle[...] + jnp.where(iota((8, width), 0) < 4, spread4, 0.0)
+        s.middle[...] = middle
+        rows4 = folded_rows(normed_rows(middle), 0).astype(BF16)
+        late.send(jnp.concatenate([rows4, s.route[...]], axis=1))
+        weights_last()
+        early.experts()
+        late.forward(0, nz)
+        early.sums()
+        late.experts()
+        late.sums()
+        first, last = late.collect(), early.collect()
+        low = jnp.where(low4, first, pltpu.roll(last, 4, 0))
+        high = jnp.where(low4, pltpu.roll(first, 4, 0), last)
+        finished(s.middle[...] + jnp.concatenate([low, high], axis=1))
 
     def f_copy(src_k, dst_k):
         start = pl.multiple_of(128 * (3 * (dst_k // 2) + lax.rem(dst_k, 2)), 128)
@@ -624,16 +757,23 @@
         peer = z_peer(d)
         q_copy(zz, peer).wait_send()
         pz_copy(zz, peer).wait_send()
-        xz_copy(zz, peer).wait_send()
-        oz_copy(zz, peer).wait_send()
 
     loop(1, nz, z_sent)
     for d in range(1, ny):
         peer = y_peer(d)
         qy_copy(yy, peer).wait_send()
         py_copy(yy, peer).wait_send()
-        loop(0, nz, lambda z: xy_copy(yy, peer, z).wait_send())
-        loop(0, groups, lambda g: oy_copy(yy, peer, g).wait_send())
+
+    @pl.when(kk != 0)
+    def _():
+        dec_copy(kk).wait_send()
+        full.finish()
+
+    @pl.when(kk == 0)
+    def _():
+        early.finish()
+        late.finish()
+
     for d in range(1, nkv):
         peer = k_peer(d)
         res_copy(kk, peer).wait_send()
@@ -656,6 +796,22 @@
 
 
 INPUTS = ("res", "q", "pre", "kv", "pt", "len", "w", "gi", "go", "ids", "rw", "st", "wgu", "wd")
+PASS_SCRATCH = (
+    "x",
+    "o",
+    "oy",
+    "os",
+    "ob",
+    "s_xz",
+    "r_xz",
+    "s_xr",
+    "s_xy",
+    "r_xy",
+    "s_oy",
+    "r_oy",
+    "s_oz",
+    "r_oz",
+)
 LOADED = ("q", "res", "gi", "go", "pre", "w", "ids", "rw", "st", "pt", "len", "kv")
 
 
@@ -715,7 +871,10 @@
         zsend=V((nz, 8, 128), BF16),
         zbuf=V((nz, 8, 128), BF16),
         pre_s=V((64, 192), F32),
-        head_rows=V((8, width), F32),
+        decsend=V((8, width // 2), BF16),
+        decbuf=V((nkv, 8, width // 2), BF16),
+        s_dec=dma(1),
+        r_dec=dma(nkv),
         proj=V((nkv, 8, width), BF16),
         rsbuf=V((nkv, 8, width), BF16),
         ressend=V((nkv, 8, 256), BF16),
@@ -727,12 +886,8 @@
         rw_t=V((128, 8), F32),
         route=V((8, 128), BF16),
         middle=V((8, width), F32),
-        gain_out=V((1, width), F32),
-        xbuf=V((ny, nz, 8, width + 128), BF16),
-        obuf=V((ny, nz, 8, width), BF16),
-        oybuf=V((ny, nz, 8, width), BF16),
-        ozsend=V((nz, 8, width), BF16),
-        ozbuf=V((nz, 8, width), BF16),
+        gains=V((8, width), F32),
+        normed=V((8, width), F32),
         fsend=V((8, width), BF16),
         fbuf=V((nkv, 8, 256), BF16),
         l_in=dma(len(LOADED)),
@@ -743,16 +898,10 @@
         r_wd=dma(nkv),
         r_fg=dma(2),
         r_fd=dma(2),
-        s_xy=dma(ny, nz),
-        r_xy=dma(ny, nz),
-        s_oy=dma(ny, groups),
-        r_oy=dma(ny, groups),
     )
     for name, n in (
         ("q", nz),
         ("pz", nz),
-        ("xz", nz),
-        ("oz", nz),
         ("qy", ny),
         ("py", ny),
         ("rs", nkv),
@@ -762,6 +911,24 @@
     ):
         scratch["s_" + name] = dma(n)
         scratch["r_" + name] = dma(n)
+    for tag, cols in (("a", width), ("b", width // 2), ("c", width // 2)):
+        shapes = dict(
+            x=V((ny, nz, 8, cols + 128), BF16),
+            o=V((ny, nz, 8, cols), BF16),
+            oy=V((ny, nz, 8, cols), BF16),
+            os=V((nz, 8, cols), BF16),
+            ob=V((nz, 8, cols), BF16),
+            s_xz=dma(nz),
+            r_xz=dma(nz),
+            s_xr=dma(8),
+            s_xy=dma(ny, nz),
+            r_xy=dma(ny, nz),
+            s_oy=dma(ny, groups),
+            r_oy=dma(ny, groups),
+            s_oz=dma(nz),
+            r_oz=dma(nz),
+        )
+        scratch.update({name + "_" + tag: shape for name, shape in shapes.items()})
     names = [name + "_in" for name in INPUTS] + ["out_v"] + list(scratch)
     return pl.pallas_call(
         functools.partial(layer_kernel, nz, nkv, names),

time: 120 us -> 96.5 us (0.80)
  Pallas kernels: 119 us -> 94.3 us
    pallas_call x1, Pallas kernels: 119 us -> 94.3 us  [local(): pl.pallas_call(functools.partial(layer_kernel, nz, nkv, names), out_shape...]
where the time goes in v3:
time: 96.5 us; the launch traced here: 95.7 us
  Pallas kernels  94.3 us (98%)
  local copies, waits for them, and re-layouts  1.38 us (1%)
    pallas_call x1, Pallas kernels, local(): pl.pallas_call(functools.partial(layer_kernel, nz, nkv, names), out_shape...  94.3 us

profile of v3, /device:TPU:1, one launch (start us, length us, event | category | flops | bytes accessed | tf_op | source)
XLA Modules:
  0.0 95.7 jit_solution(13485705126074410060)
XLA Ops:
  0.0 94.3 %layer.1 = bf16[64,192]{1,0:T(8,128)(2,1)} custom-call(bf16[64,192]{1,0:T(8,128)(2,1)} %refs_0_.1, bf16[4,192]{1,0:T(4,128)(2,1)} %refs_1_.1, bf16[60,192]{1,0:T(8,128)(2,1)} %refs_2_.1, bf16[16,128,128]{2,1,0:T(8,128)(2,1)} %bitcast.9, s32[4,256]{1,0:T(4,128)} %bitcast.11, s32[1,256]{1,0:T(1,128)} %bitcast.14, bf16[192,1536]{1,0:T(8,128)(2,1)} %refs_6_.1, ...), custom_call_target="tpu_custom_call" | custom-call | tf_op jit(solution)/shard_map/layer/pallas_call | solution.py:933
  94.3 1.4 %copy.16 = bf16[64,192]{1,0:T(8,128)(2,1)} copy(bf16[64,192]{1,0:T(8,128)(2,1)} %layer.1) | data formatting | bytes 49152

commit v4 on v3

--- a/solution.py
+++ b/solution.py
@@ -401,9 +401,11 @@
             mine = jnp.where(iota(share.shape, 1) % 64 == pg, share, 0.0)
             return produced.astype(BF16).astype(F32) * jnp.sum(mine, axis=1, keepdims=True)
 
-        def experts_of(y):
-            x = p.x[y].reshape(nz * 8, cols + 128)
-            p.o[y] = mlp(x[:, :cols], x[:, cols:].astype(F32)).astype(BF16).reshape(nz, 8, cols)
+        def experts_of_both(ya, yb):
+            x = jnp.concatenate([p.x[y].reshape(nz * 8, cols + 128) for y in (ya, yb)], axis=0)
+            out = mlp(x[:, :cols], x[:, cols:].astype(F32)).astype(BF16)
+            p.o[ya] = out[: nz * 8].reshape(nz, 8, cols)
+            p.o[yb] = out[nz * 8 :].reshape(nz, 8, cols)
 
         def experts_of_pair(ya, yb):
             n = nz * 8
@@ -430,18 +432,13 @@
                     oy_copy(yy, y_peer(d), nth_group(g)).start()
 
         def experts():
-            for pair in ((0, 1), (3, 2)):
-                if folded:
-                    arrived(pair[0])
-                    arrived(pair[1])
-                    experts_of_pair(y_peer(pair[0]), y_peer(pair[1]))
-                    go_back(pair[0])
-                    go_back(pair[1])
-                else:
-                    for d in pair:
-                        arrived(d)
-                        experts_of(y_peer(d))
-                        go_back(d)
+            compute = experts_of_pair if folded else experts_of_both
+            for pair in ((1, 3), (2, 0)):
+                for d in pair:
+                    arrived(d)
+                compute(y_peer(pair[0]), y_peer(pair[1]))
+                for d in pair:
+                    go_back(d)
 
         def sums():
             for g in order:
@@ -540,6 +537,15 @@
     wanted = 8.0 * owner_pg + (owner - 4.0 * owner_pg) + jnp.where(head == 2, 4.0, 0.0)
     select = (iota((rows, npg * 8), 1).astype(F32) == wanted) & (head < 3)
     s.select[...] = select.astype(BF16)
+    eye = iota((rows, rows), 0) == iota((rows, rows), 1)
+    owner_row = jnp.sum(jnp.where(eye, owner, 0.0), axis=0, keepdims=True)
+    s.owner_row[...] = owner_row
+    out_row = iota((npg * 8, rows), 0)
+    request = ((out_row // 8) * 4 + out_row % 4).astype(F32)
+    side = (out_row // 4) % 2
+    head_all = iota((npg * 8, rows), 1) % 8
+    scatter = (request == owner_row) & (head_all // 2 == side)
+    s.scatter[...] = scatter.astype(BF16)
 
     pl.semaphore_wait(barrier, callers)
     loop(1, nz, lambda d: q_copy(zz, z_peer(nz - d)).start())
@@ -610,7 +616,7 @@
     acc = acc / jnp.where(alive, total, 1.0)
 
     eye = iota((rows, rows), 0) == iota((rows, rows), 1)
-    owner_row = jnp.sum(jnp.where(eye, owner, 0.0), axis=0, keepdims=True)
+    owner_row = s.owner_row[...]
     lse_row = jnp.sum(jnp.where(eye, lse, 0.0), axis=0, keepdims=True)
     head_row = iota((1, rows), 1) % 8
     group = (owner == owner_row) & (head == head_row) & (lse_row > -1e29)
@@ -641,13 +647,8 @@
     placed = jnp.where(head == 3, stats, placed)
     placed_hi = placed.astype(BF16)
     placed_lo = (placed - placed_hi.astype(F32)).astype(BF16)
-    out_row = iota((npg * 8, rows), 0)
-    request = ((out_row // 8) * 4 + out_row % 4).astype(F32)
-    side = (out_row // 4) % 2
-    head_all = iota((npg * 8, rows), 1) % 8
-    scatter = (request == owner_row) & (head_all // 2 == side)
     scattered = jnp.dot(
-        scatter.astype(BF16),
+        s.scatter[...],
         jnp.concatenate([placed_hi, placed_lo], axis=1),
         preferred_element_type=F32,
     )
@@ -683,11 +684,6 @@
     loop(1, nz, lambda i: pz_copy(zz, nth_z(nz - i)).start())
     s.zbuf[zz] = s.zsend[zz]
     weights_middle()
-
-    @pl.when(kk > 0)
-    def _():
-        if nz > near_half:
-            full.forward(near_half, nz)
 
     @pl.when(kk == 0)
     def _():
@@ -712,6 +708,8 @@
     @pl.when(kk != 0)
     def _():
         dec_copy(kk).start()
+        if nz > near_half:
+            full.forward(near_half, nz)
         weights_last()
         full.experts()
         full.sums()
@@ -867,6 +865,8 @@
         qall=V((ny, nz, 8, 128), BF16),
         select=V((by_name["kv"].shape[0] * 8, npg * 8), BF16),
         part=V((ny, nz, 8, 128), BF16),
+        scatter=V((npg * 8, by_name["kv"].shape[0] * 8), BF16),
+        owner_row=V((1, by_name["kv"].shape[0] * 8), F32),
         ybuf=V((ny, nz, 8, 128), BF16),
         zsend=V((nz, 8, 128), BF16),
         zbuf=V((nz, 8, 128), BF16),

time: 96.5 us -> 95.7 us (level)
  no operation moved by 1% of the time
where the time goes in v4:
time: 95.7 us; the launch traced here: 95.2 us
  Pallas kernels  93.9 us (98%)
  local copies, waits for them, and re-layouts  1.38 us (1%)
    pallas_call x1, Pallas kernels, local(): pl.pallas_call(functools.partial(layer_kernel, nz, nkv, names), out_shape...  93.9 us

profile of v4, /device:TPU:1, one launch (start us, length us, event | category | flops | bytes accessed | tf_op | source)
XLA Modules:
  0.0 95.2 jit_solution(16846674455516495611)
XLA Ops:
  0.0 93.9 %layer.1 = bf16[64,192]{1,0:T(8,128)(2,1)} custom-call(bf16[64,192]{1,0:T(8,128)(2,1)} %refs_0_.1, bf16[4,192]{1,0:T(4,128)(2,1)} %refs_1_.1, bf16[60,192]{1,0:T(8,128)(2,1)} %refs_2_.1, bf16[16,128,128]{2,1,0:T(8,128)(2,1)} %bitcast.9, s32[4,256]{1,0:T(4,128)} %bitcast.11, s32[1,256]{1,0:T(1,128)} %bitcast.14, bf16[192,1536]{1,0:T(8,128)(2,1)} %refs_6_.1, ...), custom_call_target="tpu_custom_call" | custom-call | tf_op jit(solution)/shard_map/layer/pallas_call | solution.py:933
  93.9 1.4 %copy.16 = bf16[64,192]{1,0:T(8,128)(2,1)} copy(bf16[64,192]{1,0:T(8,128)(2,1)} %layer.1) | data formatting | bytes 49152

commit v5 on v4

--- a/solution.py
+++ b/solution.py
@@ -159,7 +159,7 @@
     s.qtile[...] = jnp.zeros_like(s.qtile)
     s.qtile[0:own_req, :] = q32[:, :128]
     s.qtile[4 : 4 + own_req, 0:64] = q32[:, 128:]
-    s.qall[yy, zz] = s.qtile[...].astype(BF16)
+    s.qall[yy, zz] = s.qtile[0:8, :].astype(BF16)
 
     def q_copy(src_z, dst_z):
         ref = s.qall.at[yy, src_z]
@@ -240,10 +240,10 @@
         .astype(BF16)
         .reshape(s.ressend.shape)
     )
-    s.gsend[...] = jnp.zeros_like(s.gsend)
-    s.gsend[0:1, 0:192] = s.gi[...]
-    s.gsend[1:2, 0:192] = s.go[...]
-    gains = s.gsend[...]
+    s.gtile[...] = jnp.zeros_like(s.gtile)
+    s.gtile[0:1, 0:192] = s.gi[...]
+    s.gtile[1:2, 0:192] = s.go[...]
+    gains = s.gtile[0:8, :]
     s.gsend[...] = jnp.where(cc == 1, pltpu.roll(gains, 64, 1), gains)
 
     def res_copy(src_k, dst_k):
@@ -262,8 +262,8 @@
     s.gbuf[kk] = s.gsend[...]
 
     s.pre_s[0:own_req, :] = jnp.zeros((own_req, s.pre_s.shape[1]), F32)
-    s.pre_s[own_req:, :] = s.pre[...].astype(F32)
-    done = jnp.dot(s.pre_s[...].astype(BF16), s.w[...], preferred_element_type=F32)
+    s.pre_s[own_req:64, :] = s.pre[...].astype(F32)
+    done = jnp.dot(s.pre_s[0:64, :].astype(BF16), s.w[...], preferred_element_type=F32)
     s.proj[...] = done.astype(BF16).reshape(s.proj.shape)
 
     def rs_copy(src_k, dst_k):
@@ -528,7 +528,7 @@
     cached_lane = s.len[...].astype(F32)
     owner, limit = jnp.zeros(wide, F32), jnp.zeros(wide, F32)
     for j in range(s.pt.shape[0]):
-        mine = s.pt[j : j + 1, :] == page_row + pg * pages
+        mine = s.pt[...][j : j + 1, :] == page_row + pg * pages
         owner = owner + jnp.where(mine, request_lane, 0.0)
         limit = limit + jnp.where(mine, cached_lane - 128.0 * j, 0.0)
     owner = jnp.sum(owner, axis=1, keepdims=True)
@@ -703,7 +703,7 @@
 
     def finished(mixed):
         square = jnp.sum(mixed * mixed, axis=1, keepdims=True) / width
-        s.fsend[...] = (mixed * lax.rsqrt(square + EPSILON) * s.gains[1:2]).astype(BF16)
+        s.fsend[...] = (mixed * lax.rsqrt(square + EPSILON) * s.gains[...][1:2]).astype(BF16)
 
     @pl.when(kk != 0)
     def _():
@@ -861,7 +861,8 @@
     scratch.update(
         wgu=V((nkv, 192, ff2), BF16),
         wd=V((nkv, 192, ff), BF16),
-        qtile=V((8, 128), F32),
+        qtile=V((16, 128), F32),
+        gtile=V((16, 256), F32),
         qall=V((ny, nz, 8, 128), BF16),
         select=V((by_name["kv"].shape[0] * 8, npg * 8), BF16),
         part=V((ny, nz, 8, 128), BF16),
@@ -870,7 +871,7 @@
         ybuf=V((ny, nz, 8, 128), BF16),
         zsend=V((nz, 8, 128), BF16),
         zbuf=V((nz, 8, 128), BF16),
-        pre_s=V((64, 192), F32),
+        pre_s=V((72, 192), F32),
         decsend=V((8, width // 2), BF16),
         decbuf=V((nkv, 8, width // 2), BF16),
         s_dec=dma(1),

time: 95.7 us -> 95.7 us (level)
  no operation moved by 1% of the time
where the time goes in v5:
time: 95.7 us; the launch traced here: 95.2 us
  Pallas kernels  93.9 us (98%)
  local copies, waits for them, and re-layouts  1.38 us (1%)
    pallas_call x1, Pallas kernels, local(): pl.pallas_call(functools.partial(layer_kernel, nz, nkv, names), out_shape...  93.9 us

profile of v5, /device:TPU:1, one launch (start us, length us, event | category | flops | bytes accessed | tf_op | source)
XLA Modules:
  0.0 95.2 jit_solution(7728442134546825439)
XLA Ops:
  0.0 93.9 %layer.1 = bf16[64,192]{1,0:T(8,128)(2,1)} custom-call(bf16[64,192]{1,0:T(8,128)(2,1)} %refs_0_.1, bf16[4,192]{1,0:T(4,128)(2,1)} %refs_1_.1, bf16[60,192]{1,0:T(8,128)(2,1)} %refs_2_.1, bf16[16,128,128]{2,1,0:T(8,128)(2,1)} %bitcast.9, s32[4,256]{1,0:T(4,128)} %bitcast.11, s32[1,256]{1,0:T(1,128)} %bitcast.14, bf16[192,1536]{1,0:T(8,128)(2,1)} %refs_6_.1, ...), custom_call_target="tpu_custom_call" | custom-call | tf_op jit(solution)/shard_map/layer/pallas_call | solution.py:934
  93.9 1.4 %copy.16 = bf16[64,192]{1,0:T(8,128)(2,1)} copy(bf16[64,192]{1,0:T(8,128)(2,1)} %layer.1) | data formatting | bytes 49152
